TPU v7x, 32 devices: a whole 2x2x4 slice. The times are simulated.
32 devices in a mesh: gx: 4 (over y, core), gy: 4 (over z), gz: 2 (over x).
Axes of the slice: x: 2, y: 2, z: 4, core: 2. Of those that a mesh axis runs over, the one named last changes fastest.
Arguments:
- right_sides: float32 [6, 128, 128, 256], P(None, 'gx', 'gy', 'gz'), may hold values from -6 to 6
- permeability: float32 [128, 128, 256], P('gx', 'gy', 'gz'), may hold values from 0.1 to 10
Outputs:
- basis_q: float32 [24, 128, 128, 256], P(None, 'gx', 'gy', 'gz')
- factor_r: float32 [24, 24], replicated
All inputs are finite; a program needn't handle non-finite values.
Results may differ from a plain program's by a relative error of at most 0.00012.
Values sent between devices are 32-bit elements; how exact they have to be, the bound alone decides.
No kernel may reach another device: no remote copies, remote signals or barrier semaphores. Data moves between devices by JAX's collectives and lax.ppermute only.
A program may use at most 128 MiB of HBM per device.

v0:
```python
import jax
import jax.numpy as jnp
from jax import lax
from jax.sharding import PartitionSpec as P


def extended(cells, sides, width):
    for axis, dim in sides:
        count = lax.axis_size(axis)
        ends = count - 1
        head = lax.slice_in_dim(cells, 0, width, axis=dim)
        tail = lax.slice_in_dim(cells, cells.shape[dim] - width, cells.shape[dim], axis=dim)
        cells = jnp.concatenate(
            [
                lax.ppermute(tail, axis, [(i, (i + 1) % count) for i in range(ends)]),
                cells,
                lax.ppermute(head, axis, [((i + 1) % count, i) for i in range(ends)]),
            ],
            axis=dim,
        )
    return cells


def face_weights(kappa_pad):
    center = kappa_pad[1:-1, 1:-1, 1:-1]
    others = [
        kappa_pad[2:, 1:-1, 1:-1],
        kappa_pad[:-2, 1:-1, 1:-1],
        kappa_pad[1:-1, 2:, 1:-1],
        kappa_pad[1:-1, :-2, 1:-1],
        kappa_pad[1:-1, 1:-1, 2:],
        kappa_pad[1:-1, 1:-1, :-2],
    ]
    face_list = []
    for neighbour in others:
        divisor = center + neighbour
        divisor = jnp.where(divisor > 0, divisor, 1.0)
        face_list.append(2.0 * center * neighbour / divisor)
    diagonal = face_list[0]
    for weight in face_list[1:]:
        diagonal = diagonal + weight
    diagonal = jnp.where(diagonal > 0, diagonal, 1.0)
    return (face_list, diagonal)


def stencil(field_pad, face_list, diagonal):
    slices = [
        field_pad[:, 2:, 1:-1, 1:-1],
        field_pad[:, :-2, 1:-1, 1:-1],
        field_pad[:, 1:-1, 2:, 1:-1],
        field_pad[:, 1:-1, :-2, 1:-1],
        field_pad[:, 1:-1, 1:-1, 2:],
        field_pad[:, 1:-1, 1:-1, :-2],
    ]
    accum = face_list[0] * slices[0]
    for weight, piece in zip(face_list[1:], slices[1:]):
        accum = accum + weight * piece
    return 2.5 * accum / diagonal


def crop_cube(array, margin):
    if margin == 0:
        return array
    return array[..., margin:-margin, margin:-margin, margin:-margin]


def lower_factor(matrix):
    order = matrix.shape[0]
    positions = jnp.arange(order)
    lower = jnp.zeros_like(matrix)
    for column in range(order):
        remain = matrix[:, column] - jnp.dot(lower, lower[column], precision=lax.Precision.HIGHEST)
        pivot = jnp.sqrt(remain[column])
        entries = jnp.where(
            positions > column, remain / pivot, jnp.where(positions == column, pivot, 0.0)
        )
        lower = lower + entries[:, None] * (positions[None, :] == column).astype(matrix.dtype)
    return lower


def lower_inverse(lower):
    order = lower.shape[0]
    positions = jnp.arange(order)
    inverse = jnp.zeros_like(lower)
    for row_index in range(order):
        unit_row = (positions == row_index).astype(lower.dtype)
        partial_row = unit_row - jnp.dot(lower[row_index], inverse, precision=lax.Precision.HIGHEST)
        new_row = partial_row / lower[row_index, row_index]
        inverse = inverse + unit_row[:, None] * new_row[None, :]
    return inverse


def on_device(right_sides, permeability):
    sides = right_sides.shape[0]
    depth = 3
    powers = [right_sides]
    stacked = jnp.concatenate([right_sides, permeability[None]], 0)
    padded = extended(stacked, (("gx", 1), ("gy", 2), ("gz", 3)), 3)
    field = padded[:sides]
    face_list, diagonal = face_weights(padded[sides])
    for power_index in range(depth):
        field = stencil(
            field,
            [crop_cube(weight, power_index) for weight in face_list],
            crop_cube(diagonal, power_index),
        )
        powers.append(crop_cube(field, depth - 1 - power_index))
    basis = jnp.concatenate(powers, 0)
    columns = basis.shape[0]
    flat = basis.reshape(columns, -1)
    cell_count = flat.shape[1] * lax.axis_size("gx") * lax.axis_size("gy") * lax.axis_size("gz")
    gram = jnp.dot(flat, flat.T, precision=lax.Precision.HIGHEST)
    total_gram = lax.psum(gram, ("gx", "gy", "gz"))
    factor_r = lower_factor(total_gram / cell_count).T
    inverse = lower_inverse(factor_r.T)
    solved = jnp.dot(inverse, flat, precision=lax.Precision.HIGHEST)
    return (solved.reshape(basis.shape), factor_r)


def solution(mesh):
    placed = (P(None, "gx", "gy", "gz"), P("gx", "gy", "gz"))
    return jax.shard_map(
        on_device,
        mesh=mesh,
        in_specs=placed,
        out_specs=(P(None, "gx", "gy", "gz"), P()),
        check_vma=False,
    )
```

profile of v0, /device:TPU:0, one launch (start us, length us, event | category | flops | bytes accessed | tf_op | source)
XLA Modules:
  0.0 402.8 jit_solution(4951736670717324421)
XLA Ops:
  0.6 4.7 %copy.17 = f32[6,32,32,128]{3,0,2,1:T(8,128)S(1)} copy(f32[6,32,32,128]{3,2,1,0:T(8,128)} %param.2) | data formatting | bytes 6291456 | tf_op args[0]
  23.4 4.4 %collective-permute-done.3 = f32[7,38,3,128]{3,0,2,1:T(8,128)S(1)} collective-permute-done((f32[7,38,3,128]{3,0,2,1:T(8,128)S(1)}, f32[7,38,3,128]{3,0,2,1:T(8,128)S(1)}, u32[]{:S(2)}, u32[]{:S(2)}) %collective-permute-start.3) | collective-permute-done | bytes 408608 | tf_op jit(solution)/shard_map/ppermute | solution.py:17
  30.7 6.3 %fusion.236 = (f32[7,38,38,3]{3,0,2,1:T(8,128)}, f32[7,38,38,3]{3,0,2,1:T(8,128)}) fusion(f32[7,38,38,128]{3,0,2,1:T(8,128)S(1)} %pad_maximum_fusion.2), kind=kLoop, calls=%fused_computation.506 | loop fusion | bytes 485184 | tf_op jit(solution)/shard_map/slice | solution.py:12
  37.0 4.7 %copy.13 = f32[7,38,38,3]{2,1,3,0:T(8,128)S(1)} copy(f32[7,38,38,3]{3,0,2,1:T(8,128)} %get-tuple-element.41) | data formatting | bytes 242592 | tf_op jit(solution)/shard_map/slice | solution.py:12
  41.7 4.7 %copy.14 = f32[7,38,38,3]{2,1,3,0:T(8,128)S(1)} copy(f32[7,38,38,3]{3,0,2,1:T(8,128)} %get-tuple-element.42) | data formatting | bytes 242592 | tf_op jit(solution)/shard_map/slice | solution.py:11
  47.8 5.5 %collective-permute-start.4 = (f32[7,38,38,3]{2,1,3,0:T(8,128)S(1)}, f32[7,38,38,3]{2,1,3,0:T(8,128)}, u32[]{:S(2)}, u32[]{:S(2)}) collective-permute-start(f32[7,38,38,3]{2,1,3,0:T(8,128)S(1)} %copy.13), channel_id=1, source_target_pairs={{0,1},{2,3},{4,5},{6,7},{8,9},{10,11},{12,13},{14,15},{16,17},{18,... | collective-permute-start | bytes 363896 | tf_op jit(solution)/shard_map/ppermute | solution.py:15
  54.5 4.6 %collective-permute-done.4 = f32[7,38,38,3]{2,1,3,0:T(8,128)} collective-permute-done((f32[7,38,38,3]{2,1,3,0:T(8,128)S(1)}, f32[7,38,38,3]{2,1,3,0:T(8,128)}, u32[]{:S(2)}, u32[]{:S(2)}) %collective-permute-start.4) | collective-permute-done | bytes 121328 | tf_op jit(solution)/shard_map/ppermute | solution.py:15
  59.0 5.4 %copy.15 = f32[7,38,38,3]{3,0,2,1:T(8,128)} copy(f32[7,38,38,3]{2,1,3,0:T(8,128)} %collective-permute-done.4) | data formatting | bytes 242592 | tf_op jit(solution)/shard_map/ppermute | solution.py:15
  64.4 4.5 %copy.16 = f32[7,38,38,3]{3,0,2,1:T(8,128)} copy(f32[7,38,38,3]{2,1,3,0:T(8,128)S(1)} %collective-permute-done.5) | data formatting | bytes 242592 | tf_op jit(solution)/shard_map/ppermute | solution.py:17
  68.9 18.4 %pad_maximum_fusion.1 = f32[7,38,38,134]{3,0,2,1:T(8,128)S(1)} fusion(f32[7,38,38,3]{3,0,2,1:T(8,128)} %copy.16, f32[7,38,3,128]{3,0,2,1:T(8,128)S(1)} %collective-permute-done.3, f32[7,3,32,128]{3,0,2,1:T(8,128)S(1)} %collective-permute-done.1, f32[1,32,32,128]{3,0,2,1:T(1,128)S(1)} %bitcast.535, f32[6,32,32,128]{3,0,2,1:T(8,128)} %copy-done.2, ...), kind=kLoop, calls=%fused_computation.4 | loop fusion | flops 9481304 | bytes 10835776 | tf_op jit(solution)/shard_map/concatenate | solution.py:13
  89.1 3.5 compare_select_fusion
  108.0 29.7 %fusion.4 = f32[6,36,36,132]{3,0,2,1:T(8,128)} fusion(f32[7,38,38,134]{3,0,2,1:T(8,128)} %copy-done, f32[36,36,132]{2,1,0:T(8,128)} %copy-done.8, f32[36,36,132]{2,1,0:T(8,128)S(1)} %get-tuple-element.38, f32[36,36,132]{2,1,0:T(8,128)} %copy-done.7, f32[36,36,132]{2,1,0:T(8,128)} %copy-done.6, f32[36,36,132]{2,1,0:T(8,128)} %copy-done.5, ...), kind=kLoop, calls=%fused_computation.8 | loop fusion | flops 13343616 | bytes 33530112 | tf_op jit(solution)/shard_map/div | solution.py:58
  140.4 6.6 %slice.691 = f32[6,32,32,128]{3,0,2,1:T(8,128)} slice(f32[6,36,36,132]{3,0,2,1:T(8,128)} %fusion.4), slice={[0:6], [2:34], [2:34], [2:130]} | slice | bytes 6291456 | tf_op jit(solution)/shard_map/slice | solution.py:64
  147.0 26.7 %fusion.11 = f32[6,34,34,130]{3,0,2,1:T(8,128)} fusion(f32[6,36,36,132]{3,0,2,1:T(8,128)} %fusion.4, f32[34,34,130]{2,1,0:T(8,128)S(1)} %copy-done.10, f32[34,34,130]{2,1,0:T(8,128)} %slice.702, f32[34,34,130]{2,1,0:T(8,128)} %slice.700, f32[34,34,130]{2,1,0:T(8,128)} %slice.698, f32[34,34,130]{2,1,0:T(8,128)} %slice.696, f32[34,34,130]{2,1,0:T(8,128)S(1)} %copy-done.11, ...), kind=kLoop, calls=%fused_computation.21 | loop fusion | flops 11721840 | bytes 29454880 | tf_op jit(solution)/shard_map/div | solution.py:58
  173.7 23.0 %fusion.235 = (f32[6,32,32,128]{3,0,2,1:T(8,128)}, f32[6,32,32,128]{3,0,2,1:T(8,128)}) fusion(f32[6,34,34,130]{3,0,2,1:T(8,128)} %fusion.11, f32[32,32,128]{2,1,0:T(8,128)S(1)} %slice.718, f32[32,32,128]{2,1,0:T(8,128)} %slice.716, f32[32,32,128]{2,1,0:T(8,128)} %slice.714, f32[32,32,128]{2,1,0:T(8,128)} %slice.712, f32[32,32,128]{2,1,0:T(8,128)} %slice.710, ...), kind=kLoop, calls=%fused_computation.505 | loop fusion | flops 10223616 | bytes 31981568 | tf_op jit(solution)/shard_map/slice | solution.py:64
  196.7 6.8 %pad_maximum_fusion = f32[24,32,32,128]{3,0,2,1:T(8,128)S(1)} fusion(f32[6,32,32,128]{3,0,2,1:T(8,128)} %get-tuple-element.40, f32[6,32,32,128]{3,0,2,1:T(8,128)} %get-tuple-element.39, f32[6,32,32,128]{3,0,2,1:T(8,128)} %slice.691, f32[6,32,32,128]{3,0,2,1:T(8,128)S(1)} %copy-done.3), kind=kLoop, calls=%fused_computation.1 | loop fusion | flops 9437184 | bytes 25165824 | tf_op jit(solution)/shard_map/concatenate | solution.py:108
  203.5 4.8 %copy-done.1 = f32[24,32,32,128]{3,0,2,1:T(8,128)} copy-done((f32[24,32,32,128]{3,0,2,1:T(8,128)}, f32[24,32,32,128]{3,0,2,1:T(8,128)S(1)}, u32[]{:S(2)}) %copy-start.1) | copy-done | bytes 12582936
  208.3 13.1 %convolution_bitcast_fusion = f32[24,24]{1,0:T(8,128)S(1)} fusion(f32[24,32,32,128]{3,0,2,1:T(8,128)S(1)} %pad_maximum_fusion), kind=kOutput, calls=%fused_computation.59 | convolution fusion | flops 905969664 | bytes 12585216 | tf_op jit(solution)/shard_map/dot_general | solution.py:112
  221.6 12.0 %copy.18 = f32[24,32,32,128]{3,2,1,0:T(8,128)} copy(f32[24,32,32,128]{3,0,2,1:T(8,128)} %copy-done.1) | data formatting | bytes 25165824 | tf_op jit(solution)/shard_map/concatenate | solution.py:108
  233.5 44.9 %psum.7 = f32[24,24]{1,0:T(8,128)S(1)} all-reduce(f32[24,24]{1,0:T(8,128)S(1)} %convolution_bitcast_fusion), channel_id=1, replica_groups=mesh['gx'=4,'gy'=4,'gz'=2] {'gx','gy','gz'}, use_global_device_ids=true, to_apply=%region_0.1 | all-reduce | flops 576 | bytes 4608 | tf_op jit(solution)/shard_map/psum | solution.py:113
  318.0 16.6 %copy.30 = f32[3,8,1024,128]{3,1,2,0:T(8,128)} copy(f32[3,8,1024,128]{3,2,1,0:T(8,128)} %bitcast.530) | data formatting | bytes 25165824
  334.7 11.5 %copy.25 = f32[3,8,1024,128]{3,2,1,0:T(8,128)} copy(f32[3,8,1024,128]{3,1,2,0:T(8,128)} %copy.30) | data formatting | bytes 25165824
  366.4 24.4 %fusion = f32[24,32,32,128]{3,0,2,1:T(8,128)} fusion(f32[32,32,128,24]{2,1,0,3:T(8,128)} %bitcast.531, f32[24,24]{1,0:T(8,128)S(1)} %multiply_add_fusion.5, f32[24]{0:T(128)S(1)} %fusion.100, f32[24]{0:T(128)S(1)} %copy-done.30, f32[24]{0:T(128)S(1)} %fusion.99, f32[24]{0:T(128)S(1)} %copy-done.29, f32[24]{0:T(128)S(1)} %fusion.98, f32[24]{0:T(128)S(1)} %copy-done.28, ...), kind=kOutput, calls=%fused_computation.2 | convolution fusion | flops 905974272 | bytes 25168896 | tf_op jit(solution)/shard_map/dot_general | solution.py:116
  390.8 11.8 %copy.20 = f32[24,32,32,128]{3,2,1,0:T(8,128)} copy(f32[24,32,32,128]{3,0,2,1:T(8,128)} %fusion) | data formatting | bytes 25165824
  (230 shorter events, 86.2 us)
Async XLA Ops:
  5.5 6.6 %collective-permute-start = (f32[7,3,32,128]{3,0,2,1:T(8,128)S(1)}, f32[7,3,32,128]{3,0,2,1:T(8,128)S(1)}, u32[]{:S(2)}, u32[]{:S(2)}) collective-permute-start(f32[7,3,32,128]{3,0,2,1:T(8,128)S(1)} %get-tuple-element.45), channel_id=1, source_target_pairs={{0,8},{8,16},{16,24},{1,9},{9,17},{17,25},{2,10},{10,18},{18,26},{... | collective-permute-start | bytes 1032200 | tf_op jit(solution)/shard_map/ppermute | solution.py:15
  8.0 5.7 %collective-permute-start.1 = (f32[7,3,32,128]{3,0,2,1:T(8,128)S(1)}, f32[7,3,32,128]{3,0,2,1:T(8,128)S(1)}, u32[]{:S(2)}, u32[]{:S(2)}) collective-permute-start(f32[7,3,32,128]{3,0,2,1:T(8,128)S(1)} %get-tuple-element.46), channel_id=1, source_target_pairs={{8,0},{16,8},{24,16},{9,1},{17,9},{25,17},{10,2},{18,10},{26,18},{... | collective-permute-start | bytes 1032200 | tf_op jit(solution)/shard_map/ppermute | solution.py:17
  13.9 9.6 %collective-permute-start.2 = (f32[7,38,3,128]{3,0,2,1:T(8,128)S(1)}, f32[7,38,3,128]{3,0,2,1:T(8,128)S(1)}, u32[]{:S(2)}, u32[]{:S(2)}) collective-permute-start(f32[7,38,3,128]{3,0,2,1:T(8,128)S(1)} %get-tuple-element.43), channel_id=1, source_target_pairs={{0,2},{2,4},{4,6},{1,3},{3,5},{5,7},{8,10},{10,12},{12,14},{9,11},... | collective-permute-start | bytes 1225736 | tf_op jit(solution)/shard_map/ppermute | solution.py:15
  17.4 10.5 %collective-permute-start.3 = (f32[7,38,3,128]{3,0,2,1:T(8,128)S(1)}, f32[7,38,3,128]{3,0,2,1:T(8,128)S(1)}, u32[]{:S(2)}, u32[]{:S(2)}) collective-permute-start(f32[7,38,3,128]{3,0,2,1:T(8,128)S(1)} %get-tuple-element.44), channel_id=1, source_target_pairs={{2,0},{4,2},{6,4},{3,1},{5,3},{7,5},{10,8},{12,10},{14,12},{11,9},... | collective-permute-start | bytes 1225736 | tf_op jit(solution)/shard_map/ppermute | solution.py:17
  46.5 17.9 %collective-permute-start.5 = (f32[7,38,38,3]{2,1,3,0:T(8,128)S(1)}, f32[7,38,38,3]{2,1,3,0:T(8,128)S(1)}, u32[]{:S(2)}, u32[]{:S(2)}) collective-permute-start(f32[7,38,38,3]{2,1,3,0:T(8,128)S(1)} %copy.14), channel_id=1, source_target_pairs={{1,0},{3,2},{5,4},{7,6},{9,8},{11,10},{13,12},{15,14},{17,16},{19,... | collective-permute-start | bytes 363896 | tf_op jit(solution)/shard_map/ppermute | solution.py:17
  47.8 11.3 %collective-permute-start.4 = (f32[7,38,38,3]{2,1,3,0:T(8,128)S(1)}, f32[7,38,38,3]{2,1,3,0:T(8,128)}, u32[]{:S(2)}, u32[]{:S(2)}) collective-permute-start(f32[7,38,38,3]{2,1,3,0:T(8,128)S(1)} %copy.13), channel_id=1, source_target_pairs={{0,1},{2,3},{4,5},{6,7},{8,9},{10,11},{12,13},{14,15},{16,17},{18,... | collective-permute-start | bytes 363896 | tf_op jit(solution)/shard_map/ppermute | solution.py:15
  221.4 67.3 %copy-start.13 = (f32[24]{0:T(128)S(1)}, f32[24]{0:T(128)}, u32[]{:S(2)}) copy-start(f32[24]{0:T(128)} %get-tuple-element.78) | copy-start | bytes 292
  221.4 68.9 %copy-start.14 = (f32[24]{0:T(128)S(1)}, f32[24]{0:T(128)}, u32[]{:S(2)}) copy-start(f32[24]{0:T(128)} %get-tuple-element.77) | copy-start | bytes 292
  221.4 70.4 %copy-start.15 = (f32[24]{0:T(128)S(1)}, f32[24]{0:T(128)}, u32[]{:S(2)}) copy-start(f32[24]{0:T(128)} %compare_convert_fusion.15) | copy-start | bytes 292
  221.4 72.0 %copy-start.16 = (f32[24]{0:T(128)S(1)}, f32[24]{0:T(128)}, u32[]{:S(2)}) copy-start(f32[24]{0:T(128)} %get-tuple-element.80) | copy-start | bytes 292
  221.4 73.5 %copy-start.17 = (f32[24]{0:T(128)S(1)}, f32[24]{0:T(128)}, u32[]{:S(2)}) copy-start(f32[24]{0:T(128)} %get-tuple-element.79) | copy-start | bytes 292
  221.4 75.1 %copy-start.18 = (f32[24]{0:T(128)S(1)}, f32[24]{0:T(128)}, u32[]{:S(2)}) copy-start(f32[24]{0:T(128)} %compare_convert_fusion.12) | copy-start | bytes 292
  221.4 76.6 %copy-start.19 = (f32[24]{0:T(128)S(1)}, f32[24]{0:T(128)}, u32[]{:S(2)}) copy-start(f32[24]{0:T(128)} %get-tuple-element.82) | copy-start | bytes 292
  221.4 78.2 %copy-start.20 = (f32[24]{0:T(128)S(1)}, f32[24]{0:T(128)}, u32[]{:S(2)}) copy-start(f32[24]{0:T(128)} %get-tuple-element.81) | copy-start | bytes 292
  221.5 79.7 %copy-start.21 = (f32[24]{0:T(128)S(1)}, f32[24]{0:T(128)}, u32[]{:S(2)}) copy-start(f32[24]{0:T(128)} %get-tuple-element.84) | copy-start | bytes 292
  221.5 81.3 %copy-start.22 = (f32[24]{0:T(128)S(1)}, f32[24]{0:T(128)}, u32[]{:S(2)}) copy-start(f32[24]{0:T(128)} %get-tuple-element.83) | copy-start | bytes 292
  221.5 82.9 %copy-start.23 = (f32[24]{0:T(128)S(1)}, f32[24]{0:T(128)}, u32[]{:S(2)}) copy-start(f32[24]{0:T(128)} %get-tuple-element.86) | copy-start | bytes 292
  221.5 84.5 %copy-start.24 = (f32[24]{0:T(128)S(1)}, f32[24]{0:T(128)}, u32[]{:S(2)}) copy-start(f32[24]{0:T(128)} %get-tuple-element.85) | copy-start | bytes 292
  221.5 86.1 %copy-start.25 = (f32[24]{0:T(128)S(1)}, f32[24]{0:T(128)}, u32[]{:S(2)}) copy-start(f32[24]{0:T(128)} %get-tuple-element.88) | copy-start | bytes 292
  221.5 87.7 %copy-start.26 = (f32[24]{0:T(128)S(1)}, f32[24]{0:T(128)}, u32[]{:S(2)}) copy-start(f32[24]{0:T(128)} %get-tuple-element.87) | copy-start | bytes 292
  221.5 89.3 %copy-start.27 = (f32[24]{0:T(128)S(1)}, f32[24]{0:T(128)}, u32[]{:S(2)}) copy-start(f32[24]{0:T(128)} %get-tuple-element.90) | copy-start | bytes 292
  221.5 90.9 %copy-start.28 = (f32[24]{0:T(128)S(1)}, f32[24]{0:T(128)}, u32[]{:S(2)}) copy-start(f32[24]{0:T(128)} %get-tuple-element.89) | copy-start | bytes 292
  221.5 92.5 %copy-start.29 = (f32[24]{0:T(128)S(1)}, f32[24]{0:T(128)}, u32[]{:S(2)}) copy-start(f32[24]{0:T(128)} %get-tuple-element.92) | copy-start | bytes 292
  221.6 94.1 %copy-start.30 = (f32[24]{0:T(128)S(1)}, f32[24]{0:T(128)}, u32[]{:S(2)}) copy-start(f32[24]{0:T(128)} %get-tuple-element.91) | copy-start | bytes 292
  (13 other events, 193.1 us)
where the time goes:
time: 410 us; the launch traced here: 403 us
  local copies, waits for them, and re-layouts  129 us (31%)
  other arithmetic  122 us (30%)
  matrix products  60.7 us (15%)
  blocking collectives  44.9 us (11%)
  between operations  17.9 us (4%)
  starting transfers between devices  15.3 us (4%)
  waiting for transfers between devices  13.1 us (3%)
    div x2, other arithmetic, stencil(): return 2.5 * accum / diagonal  56.4 us
    unnamed x67, local copies, waits for them, and re-layouts  49.6 us
    psum x1, blocking collectives, on_device(): total_gram = lax.psum(gram, ('gx', 'gy', 'gz'))  44.9 us
    slice x15, local copies, waits for them, and re-layouts, crop_cube(): return array[..., margin:-margin, margin:-margin, margin:-margin]  24.5 us
    dot_general x1, matrix products, on_device(): solved = jnp.dot(inverse, flat, precision=lax.Precision.HIGHEST)  24.4 us
    slice x1, other arithmetic, crop_cube(): return array[..., margin:-margin, margin:-margin, margin:-margin]  23 us
    concatenate x2, other arithmetic, extended(): jnp.concatenate([lax.ppermute(tail, axis, [(i, (i + 1) % count) for i in...  21.2 us
    dot_general x24, matrix products, lower_inverse(): jnp.dot(lower[row_index], inverse, precision=lax.Precision.HIGHEST)  19.8 us
  transfers between devices with their start and end apart: 6, of which 4 were waited for; matrix products, arithmetic and copies ran while one was open for 3% of the time, Pallas kernels for 0%

commit v1 on v0

v1 whole, which is shorter than its diff:
```python
import functools

import jax
import jax.numpy as jnp
from jax import lax
from jax.experimental import pallas as pl
from jax.experimental.pallas import tpu as pltpu
from jax.sharding import PartitionSpec as P

F32 = jnp.float32
BF16 = jnp.bfloat16
DEPTH = 3
LANES = 128
TOP = 8
MIB = 1 << 20


def even_on(axis):
    return lax.rem(lax.axis_index(axis), 2) == 0


def lane_index(rows=8):
    return lax.broadcasted_iota(jnp.int32, (rows, LANES), 1)


def take_lanes(tile, lanes):
    return jnp.take_along_axis(tile, lanes, axis=1)


def pair_exchange(first, second, axis):
    count = lax.axis_size(axis)
    firsts = [(i, i + 1) for i in range(0, count - 1, 2)]
    seconds = [(i, i + 1) for i in range(1, count - 1, 2)]
    got_first = lax.ppermute(first, axis, [p for a, b in firsts for p in ((a, b), (b, a))])
    if not seconds:
        return (got_first,)
    got_second = lax.ppermute(second, axis, [p for a, b in seconds for p in ((a, b), (b, a))])
    return (got_first, got_second)


def pack_faces(rs_ref, k_ref, pad_ref, xa_ref, xb_ref, ya_ref, yb_ref, sems):
    fields = rs_ref.shape[0]
    nx, ny = k_ref.shape[0], k_ref.shape[1]
    copies = [
        pltpu.make_async_copy(
            rs_ref.at[f], pad_ref.at[f, pl.ds(DEPTH, nx), pl.ds(TOP, ny)], sems.at[f]
        )
        for f in range(fields)
    ]
    copies.append(
        pltpu.make_async_copy(
            k_ref, pad_ref.at[fields, pl.ds(DEPTH, nx), pl.ds(TOP, ny)], sems.at[fields]
        )
    )
    for copy in copies:
        copy.start()
    ex, ey = even_on("gx"), even_on("gy")
    start_a = jnp.where(ex, nx, DEPTH)
    start_b = jnp.where(ex, DEPTH, nx)
    for f in range(fields + 1):
        copies[f].wait()
        for i in range(DEPTH):
            xa_ref[f, i] = pad_ref[f, start_a + i, TOP : TOP + ny, :]
            xb_ref[f, i] = pad_ref[f, start_b + i, TOP : TOP + ny, :]
        for x in range(nx):
            low = pad_ref[f, x + DEPTH, TOP : TOP + DEPTH, :]
            high = pad_ref[f, x + DEPTH, TOP + ny - DEPTH : TOP + ny, :]
            row = DEPTH * (f * nx + x)
            ya_ref[row : row + DEPTH, :] = jnp.where(ey, high, low)
            yb_ref[row : row + DEPTH, :] = jnp.where(ey, low, high)


def pack_edges(xa_ref, xb_ref, ea_ref, eb_ref):
    fields, _, ny, _ = xa_ref.shape
    ex, ey = even_on("gx"), even_on("gy")
    for f in range(fields):
        for side in range(2):
            for i in range(DEPTH):
                a, b = xa_ref, xb_ref
                if side == 0:
                    low = jnp.where(ex, b[f, i, :DEPTH, :], a[f, i, :DEPTH, :])
                    high = jnp.where(ex, b[f, i, ny - DEPTH :, :], a[f, i, ny - DEPTH :, :])
                else:
                    low = jnp.where(ex, a[f, i, :DEPTH, :], b[f, i, :DEPTH, :])
                    high = jnp.where(ex, a[f, i, ny - DEPTH :, :], b[f, i, ny - DEPTH :, :])
                row = DEPTH * ((f * 2 + side) * DEPTH + i)
                ea_ref[row : row + DEPTH, :] = jnp.where(ey, high, low)
                eb_ref[row : row + DEPTH, :] = jnp.where(ey, low, high)


def assemble(nx, ny, two_z, pad_in, xa, xb, ya, yb, ea, eb, *outs):
    del pad_in
    if two_z:
        pad, own, za, zb = outs
    else:
        pad, own, za = outs
        zb = None
    slabs = pad.shape[0]
    ex, ey, ez = even_on("gx"), even_on("gy"), even_on("gz")
    bottom = TOP + ny
    wide = nx + 2 * DEPTH
    half = wide // 2
    tiles = (ny + 2 * DEPTH + 7) // 8
    for f in range(slabs):
        for i in range(DEPTH):
            a, b = xa[f, i], xb[f, i]
            pad[f, i, TOP:bottom, :] = jnp.where(ex, b, a)
            pad[f, nx + DEPTH + i, TOP:bottom, :] = jnp.where(ex, a, b)
        for x in range(nx):
            row = DEPTH * (f * nx + x)
            a, b = ya[row : row + DEPTH, :], yb[row : row + DEPTH, :]
            pad[f, x + DEPTH, TOP - DEPTH : TOP, :] = jnp.where(ey, b, a)
            pad[f, x + DEPTH, bottom : bottom + DEPTH, :] = jnp.where(ey, a, b)
        for side in range(2):
            for i in range(DEPTH):
                row = DEPTH * ((f * 2 + side) * DEPTH + i)
                plane = i if side == 0 else nx + DEPTH + i
                a, b = ea[row : row + DEPTH, :], eb[row : row + DEPTH, :]
                pad[f, plane, TOP - DEPTH : TOP, :] = jnp.where(ey, b, a)
                pad[f, plane, bottom : bottom + DEPTH, :] = jnp.where(ey, a, b)

    lane = lane_index()
    place = lane // 2
    is_left = lane % 2 == 1
    column = lane % wide
    step = jnp.minimum(lane // wide, DEPTH - 1)

    def from_halves(first, second, at, zs):
        in_first = at < half
        index = 6 * jnp.where(in_first, at, jnp.minimum(at - half, half - 1)) + zs
        return jnp.where(in_first, take_lanes(first, index), take_lanes(second, index))

    @pl.loop(0, slabs)
    def _(f):
        for t in range(tiles):
            rows = slice(TOP - DEPTH + 8 * t, TOP - DEPTH + 8 * t + 8)
            packed = []
            for part in range(2):
                acc = jnp.zeros((8, LANES), F32)
                for m in range(half):
                    tile = pad[f, part * half + m, rows, :]
                    moved = pltpu.roll(tile, 6 * m + 3, 1)
                    acc = jnp.where(lane // 6 == m, moved, acc)
                packed.append(acc)
            first, second = packed
            out = slice(8 * t, 8 * t + 8)
            for j in range(2):
                own[f, j, out, :] = from_halves(
                    first, second, place, jnp.where(is_left, 3 + j, 2 - j)
                )
            to_left, to_right = 3 + step, 2 - step
            za[f, out, :] = from_halves(first, second, column, jnp.where(ez, to_right, to_left))
            if two_z:
                zb[f, out, :] = from_halves(
                    first, second, column, jnp.where(ez, to_left, to_right)
                )


def face(center, other):
    total = center + other
    return 2.0 * center * other / jnp.where(total > 0, total, 1.0)


def scaled_faces(center, others):
    faces = [face(center, other) for other in others]
    diagonal = faces[0]
    for weight in faces[1:]:
        diagonal = diagonal + weight
    scale = 2.5 / jnp.where(diagonal > 0, diagonal, 1.0)
    return [weight * scale for weight in faces]


def weighted(weights, values):
    accum = weights[0] * values[0]
    for weight, value in zip(weights[1:], values[1:]):
        accum = accum + weight * value
    return accum


def powers(nx, ny, two_z, pad, own, za, *rest):
    if two_z:
        zb, rest = rest[0], rest[1:]
    else:
        zb = None
    high_ref, low_ref, gram_ref, coef, v1, v2, strip, scoef, s1, s2, acc, square = rest
    fields = pad.shape[0] - 1
    wide = nx + 2 * DEPTH
    ez = even_on("gz")
    lane = lane_index()
    place = lane // 2
    is_left = lane % 2 == 1
    tiles = (ny + 2 * DEPTH + 7) // 8

    @pl.loop(0, fields + 1)
    def _(f):
        for t in range(tiles):
            rows = slice(8 * t, 8 * t + 8)
            got_a = za[f, rows, :]
            if two_z:
                got_b = zb[f, rows, :]
                left = jnp.where(ez, got_b, got_a)
                right = jnp.where(ez, got_a, got_b)
            for q in range(DEPTH):
                index = jnp.minimum(wide * (DEPTH - 1 - q) + place, LANES - 1)
                if two_z:
                    tile = jnp.where(is_left, take_lanes(left, index), take_lanes(right, index))
                else:
                    keep = is_left != ez
                    tile = jnp.where(keep, take_lanes(got_a, index), 0.0)
                strip[f, q, rows, :] = tile
            for j in range(2):
                strip[f, DEPTH + j, rows, :] = own[f, j, rows, :]

    def strip_neighbours(ref, f, q, base, row):
        rows = slice(row, row + 8)
        tile = ref[f, q - base, rows, :]
        return tile, [
            pltpu.roll(tile, LANES - 2, 1),
            pltpu.roll(tile, 2, 1),
            ref[f, q - base, row + 1 : row + 9, :],
            ref[f, q - base, row - 1 : row + 7, :],
            ref[f, q + 1 - base, rows, :],
            ref[f, q - 1 - base, rows, :],
        ]

    for q in range(1, 4):
        for t in range(tiles):
            row = 1 + 8 * t
            center, others = strip_neighbours(strip, fields, q, 0, row)
            for n, weight in enumerate(scaled_faces(center, others)):
                scoef[n, q - 1, row : row + 8, :] = weight

    @pl.loop(0, fields)
    def _(f):
        for q in range(1, 4):
            for t in range(tiles):
                row = 1 + 8 * t
                weights = [scoef[n, q - 1, row : row + 8, :] for n in range(6)]
                _, values = strip_neighbours(strip, f, q, 0, row)
                s1[f, q - 1, row : row + 8, :] = weighted(weights, values)
        for t in range(tiles):
            row = 2 + 8 * t
            weights = [scoef[n, 1, row : row + 8, :] for n in range(6)]
            _, values = strip_neighbours(s1, f, 2, 1, row)
            s2[f, row : row + 8, :] = weighted(weights, values)

    def z_pair(tile, edge, plane):
        moved = pltpu.roll(edge, LANES - 1 - 2 * plane, 1)
        return [
            jnp.where(lane == LANES - 1, moved, pltpu.roll(tile, LANES - 1, 1)),
            jnp.where(lane == 0, moved, pltpu.roll(tile, 1, 1)),
        ]

    @pl.loop(0, nx + 4)
    def _(i):
        plane = i + 1
        for t in range(tiles):
            y = 8 * t - 2
            r = TOP + y
            tile = pad[fields, plane, r : r + 8, :]
            others = [
                pad[fields, plane + 1, r : r + 8, :],
                pad[fields, plane - 1, r : r + 8, :],
                pad[fields, plane, r + 1 : r + 9, :],
                pad[fields, plane, r - 1 : r + 7, :],
            ] + z_pair(tile, strip[fields, 2, y + 3 : y + 11, :], plane)
            for n, weight in enumerate(scaled_faces(tile, others)):
                coef[n, i, 8 * t : 8 * t + 8, :] = weight

    def advance(source, source_x, edge, f, plane, y, weights):
        r = TOP + y
        s = plane - source_x
        tile = source[f, s, r : r + 8, :]
        values = [
            source[f, s + 1, r : r + 8, :],
            source[f, s - 1, r : r + 8, :],
            source[f, s, r + 1 : r + 9, :],
            source[f, s, r - 1 : r + 7, :],
        ] + z_pair(tile, edge, plane)
        return weighted(weights, values)

    def weights_at(plane, y):
        return [coef[n, plane - 1, y + 2 : y + 10, :] for n in range(6)]

    @pl.loop(1, nx + 5)
    def _(plane):
        for t in range(tiles):
            y = 8 * t - 2
            weights = weights_at(plane, y)
            for f in range(fields):
                edge = strip[f, 2, y + 3 : y + 11, :]
                v1[f, plane - 1, TOP + y : TOP + y + 8, :] = advance(
                    pad, 0, edge, f, plane, y, weights
                )

    @pl.loop(2, nx + 4)
    def _(plane):
        for t in range(tiles):
            y = 8 * t - 1
            weights = weights_at(plane, y)
            for f in range(fields):
                edge = s1[f, 1, y + 3 : y + 11, :]
                v2[f, plane - 2, TOP + y : TOP + y + 8, :] = advance(
                    v1, 1, edge, f, plane, y, weights
                )

    blocks = ny // 8

    def last_power(plane):
        for t in range(blocks):
            y = 8 * t
            rows = slice(TOP + y, TOP + y + 8)
            weights = weights_at(plane, y)
            columns = [pad[f, plane, rows, :] for f in range(fields)]
            columns += [v1[f, plane - 1, rows, :] for f in range(fields)]
            columns += [v2[f, plane - 2, rows, :] for f in range(fields)]
            for f in range(fields):
                edge = s2[f, y + 3 : y + 11, :]
                columns.append(advance(v2, 2, edge, f, plane, y, weights))
            block = (plane - DEPTH) * blocks + t
            for g in range(len(columns) // 2):
                pair = jnp.concatenate(columns[2 * g : 2 * g + 2], 0)
                high = pair.astype(BF16)
                high_ref[block, 16 * g : 16 * g + 16, :] = high
                low_ref[block, 16 * g : 16 * g + 16, :] = (pair - high.astype(F32)).astype(BF16)

    def products(plane):
        base = (plane - DEPTH) * blocks
        high = jnp.concatenate([high_ref[base + t] for t in range(blocks)], 1)
        low = jnp.concatenate([low_ref[base + t] for t in range(blocks)], 1)
        both = jnp.concatenate([high, low], 0)
        acc[...] += lax.dot_general(
            both, high, (((1,), (1,)), ((), ())), preferred_element_type=F32
        )

    acc[...] = jnp.zeros_like(acc)
    last_power(DEPTH)

    @pl.loop(DEPTH + 1, nx + DEPTH)
    def _(plane):
        last_power(plane)
        products(plane - 1)

    products(nx + DEPTH - 1)

    rows = acc.shape[1]
    sums = acc[...]
    same = lax.broadcasted_iota(jnp.int32, sums.shape, 0) % 8 == (
        lax.broadcasted_iota(jnp.int32, sums.shape, 1) % 8
    )
    sums = jnp.where(same, sums, 0.0).reshape(2 * rows // 8, 8, rows).sum(1)
    pick = lax.broadcasted_iota(jnp.int32, (rows, LANES), 0) // 8 == (
        lax.broadcasted_iota(jnp.int32, (rows, LANES), 1)
    )
    small = jnp.dot(sums, pick.astype(F32), precision=lax.Precision.HIGHEST)
    order = rows // 8
    square[...] = jnp.zeros_like(square)
    square[0:order, :] = small[order : 2 * order, :]
    cross = small[order : 2 * order, :]
    gram_ref[...] = small[0:order, :] + cross + square[...].T[0:order, :]


def factor_and_solve(cells, order, ny, gram_a, gram_b, high_ref, low_ref, out_ref, factor_ref, w_wide, w_low):
    blocks = ny // 8
    rows = 8 * order

    @pl.when(pl.program_id(0) == 0)
    def _():
        row = lax.broadcasted_iota(jnp.int32, (order, LANES), 0)
        lane = lax.broadcasted_iota(jnp.int32, (order, LANES), 1)
        work = (gram_a[...] + gram_b[...]) / cells
        work = jnp.where(lane < order, work, jnp.where(lane == row + 64, 1.0, 0.0))
        for j in range(order):
            pivot = work[j : j + 1, :]
            factor = work[:, j : j + 1] / work[j : j + 1, j : j + 1]
            work = work - jnp.where(row > j, factor * pivot, 0.0)
        pivots = jnp.sum(jnp.where(lane == row, work, 0.0), 1, keepdims=True)
        work = work / jnp.sqrt(pivots)
        factor_ref[...] = jnp.where(lane >= row, work, 0.0)[:, :order]
        inverse = pltpu.roll(work, 64, 1)
        inverse = jnp.where(lane <= row, inverse, 0.0)
        high = inverse.astype(BF16)
        low = (inverse - high.astype(F32)).astype(BF16)
        spread = (
            lax.broadcasted_iota(jnp.int32, (rows, order), 0) // 8
            == lax.broadcasted_iota(jnp.int32, (rows, order), 1)
        ).astype(BF16)
        across = (
            lax.broadcasted_iota(jnp.int32, (LANES, rows), 1) // 8
            == lax.broadcasted_iota(jnp.int32, (LANES, rows), 0)
        ).astype(BF16)
        same = lax.broadcasted_iota(jnp.int32, (rows, rows), 0) % 8 == (
            lax.broadcasted_iota(jnp.int32, (rows, rows), 1) % 8
        )

        def kron(small):
            tall = jnp.dot(spread, small, preferred_element_type=F32).astype(BF16)
            full = jnp.dot(tall, across, preferred_element_type=F32)
            return jnp.where(same, full, 0.0).astype(BF16)

        w_high = kron(high)
        w_wide[:, :rows] = w_high
        w_wide[:, rows:] = w_high
        w_low[...] = kron(low)

    base = pl.program_id(0) * blocks
    high = jnp.concatenate([high_ref[base + t] for t in range(blocks)], 1)
    low = jnp.concatenate([low_ref[base + t] for t in range(blocks)], 1)
    both = jnp.concatenate([high, low], 0)
    result = jnp.dot(w_wide[...], both, preferred_element_type=F32)
    result = result + jnp.dot(w_low[...], high, preferred_element_type=F32)
    for t in range(blocks):
        for b in range(order):
            out_ref[b, 0, 8 * t : 8 * t + 8, :] = result[
                8 * b : 8 * b + 8, LANES * t : LANES * t + LANES
            ]


VM = functools.partial(pl.BlockSpec, memory_space=pltpu.VMEM)


def params(limit):
    return pltpu.CompilerParams(vmem_limit_bytes=limit * MIB)


def on_device(right_sides, permeability):
    fields, nx, ny, nz = right_sides.shape
    slabs = fields + 1
    order = fields * (DEPTH + 1)
    rows = 8 * order
    tall = ny + 16
    wide = nx + 2 * DEPTH
    strip_rows = 8 * ((ny + 2 * DEPTH + 7) // 8)
    two_z = lax.axis_size("gz") > 2
    devices = lax.axis_size("gx") * lax.axis_size("gy") * lax.axis_size("gz")
    cells = float(nx * ny * nz * devices)

    pad_type = pltpu.VMEM((slabs, wide, tall, LANES), F32)
    x_type = pltpu.VMEM((slabs, DEPTH, ny, LANES), F32)
    y_type = pltpu.VMEM((slabs * nx * DEPTH, LANES), F32)
    e_rows = 8 * ((slabs * 2 * DEPTH * DEPTH + 7) // 8)
    e_type = pltpu.VMEM((e_rows, LANES), F32)
    pad, xa, xb, ya, yb = pl.pallas_call(
        pack_faces,
        out_shape=(pad_type, x_type, x_type, y_type, y_type),
        in_specs=[pl.BlockSpec(memory_space=pl.ANY)] * 2,
        out_specs=(VM(),) * 5,
        scratch_shapes=[pltpu.SemaphoreType.DMA((slabs,))],
        compiler_params=params(8),
        name="pack_faces",
    )(right_sides, permeability)
    got_xa, got_xb = pair_exchange(xa, xb, "gx")
    got_ya, got_yb = pair_exchange(ya, yb, "gy")
    ea, eb = pl.pallas_call(
        pack_edges,
        out_shape=(e_type, e_type),
        in_specs=[VM()] * 2,
        out_specs=(VM(),) * 2,
        compiler_params=params(8),
        name="pack_edges",
    )(got_xa, got_xb)
    got_ea, got_eb = pair_exchange(ea, eb, "gy")

    own_type = pltpu.VMEM((slabs, 2, strip_rows, LANES), F32)
    z_type = pltpu.VMEM((slabs, strip_rows, LANES), F32)
    z_count = 2 if two_z else 1
    outs = pl.pallas_call(
        functools.partial(assemble, nx, ny, two_z),
        out_shape=(pad_type, own_type) + (z_type,) * z_count,
        in_specs=[VM()] * 7,
        out_specs=(VM(),) * (2 + z_count),
        input_output_aliases={0: 0},
        compiler_params=params(8),
        name="assemble",
    )(pad, got_xa, got_xb, got_ya, got_yb, got_ea, got_eb)
    pad, own = outs[:2]
    got_z = pair_exchange(outs[2], outs[-1], "gz")

    blocks = nx * ny // 8
    split_type = pltpu.VMEM((blocks, rows, LANES), BF16)
    high, low, gram = pl.pallas_call(
        functools.partial(powers, nx, ny, two_z),
        out_shape=(split_type, split_type, pltpu.VMEM((order, LANES), F32)),
        in_specs=[VM()] * (2 + len(got_z)),
        out_specs=(VM(),) * 3,
        scratch_shapes=[
            pltpu.VMEM((6, nx + 4, tall, LANES), F32),
            pltpu.VMEM((fields, nx + 4, tall, LANES), F32),
            pltpu.VMEM((fields, nx + 2, tall, LANES), F32),
            pltpu.VMEM((slabs, 5, tall, LANES), F32),
            pltpu.VMEM((6, 3, tall, LANES), F32),
            pltpu.VMEM((fields, 3, tall, LANES), F32),
            pltpu.VMEM((fields, tall, LANES), F32),
            pltpu.VMEM((2 * rows, rows), F32),
            pltpu.VMEM((LANES, LANES), F32),
        ],
        compiler_params=params(26),
        name="powers",
    )(pad, own, *got_z)

    stages = []
    for axis in ("gz", "gx", "gy"):
        count, stride = lax.axis_size(axis), 1
        while stride < count:
            stages.append((axis, [(i, i ^ stride) for i in range(count)]))
            stride *= 2
    for axis, pairs in stages[:-1]:
        gram = gram + lax.ppermute(gram, axis, pairs)
    other = lax.ppermute(gram, *stages[-1])

    basis_q, factor_r = pl.pallas_call(
        functools.partial(factor_and_solve, cells, order, ny),
        grid=(nx,),
        out_shape=(
            jax.ShapeDtypeStruct((order, nx, ny, nz), F32),
            jax.ShapeDtypeStruct((order, order), F32),
        ),
        in_specs=[VM()] * 4,
        out_specs=(
            pl.BlockSpec((order, 1, ny, nz), lambda i: (0, i, 0, 0)),
            pl.BlockSpec((order, order), lambda i: (0, 0)),
        ),
        scratch_shapes=[pltpu.VMEM((rows, 2 * rows), BF16), pltpu.VMEM((rows, rows), BF16)],
        compiler_params=params(16),
        name="factor_and_solve",
    )(gram, other, high, low)
    return (basis_q, factor_r)


def solution(mesh):
    placed = (P(None, "gx", "gy", "gz"), P("gx", "gy", "gz"))
    return jax.shard_map(
        on_device,
        mesh=mesh,
        in_specs=placed,
        out_specs=(P(None, "gx", "gy", "gz"), P()),
        check_vma=False,
    )
```

time: 410 us -> 95.3 us (0.23); the launches traced: 403 us -> 95.1 us
  local copies, waits for them, and re-layouts: 129 us -> 2.92 us
  other arithmetic: 122 us -> 0.01 us
  matrix products: 60.7 us -> 0 us
  Pallas kernels: 0 us -> 52.2 us
  blocking collectives: 44.9 us -> 0 us
  between operations: 17.9 us -> 0.71 us
  starting transfers between devices: 15.3 us -> 25.4 us
    dot_general x50 -> x0, matrix products: 60.7 us -> none  [the longest x1 24.4 us: on_device(): solved = jnp.dot(inverse, flat, precision=lax.Precision.HIGHEST)]
    slice x46 -> x0, local copies, waits for them, and re-layouts: 57.8 us -> none  [the longest x15 24.5 us: crop_cube(): return array[..., margin:-margin, margin:-margin, margin:-margin]]
    div x3 -> x0, other arithmetic: 56.4 us -> none  [the longest x2 56.4 us: stencil(): return 2.5 * accum / diagonal]
    pallas_call x0 -> x5, Pallas kernels: none -> 52.2 us  [the longest x1 27.8 us: on_device(): pl.pallas_call(functools.partial(powers, nx, ny, two_z), out_shape=(split...]
    unnamed x67 -> x4, local copies, waits for them, and re-layouts: 49.6 us -> 2.92 us
    psum x1 -> x0, blocking collectives: 44.9 us -> none  [on_device(): total_gram = lax.psum(gram, ('gx', 'gy', 'gz'))]
    concatenate x3 -> x0, other arithmetic: 28 us -> none  [the longest x2 21.2 us: extended(): jnp.concatenate([lax.ppermute(tail, axis, [(i, (i + 1) % count) for i in...]
    slice x3 -> x0, other arithmetic: 23.4 us -> none  [the longest x1 23 us: crop_cube(): return array[..., margin:-margin, margin:-margin, margin:-margin]]
  transfers between devices with their start and end apart: 6 -> 12, of which waited for: 4 -> 8; matrix products, arithmetic and copies ran while one was open for 3% -> 0% of each run, Pallas kernels for 0% -> 0%
where the time goes in v1:
time: 95.3 us; the launch traced here: 95.1 us
  Pallas kernels  52.2 us (55%)
  starting transfers between devices  25.4 us (27%)
  waiting for transfers between devices  13.8 us (14%)
  local copies, waits for them, and re-layouts  2.92 us (3%)
    pallas_call x1, Pallas kernels, on_device(): pl.pallas_call(functools.partial(powers, nx, ny, two_z), out_shape=(split...  27.8 us
    pallas_call x1, Pallas kernels, on_device(): pl.pallas_call(functools.partial(factor_and_solve, cells, order, ny), gri...  19.6 us
    ppermute x4, starting transfers between devices, pair_exchange(): lax.ppermute(first, axis, [p for a, b in firsts for p in ((a, b), (b, a))])  9.94 us
    ppermute x4, starting transfers between devices, on_device(): gram = gram + lax.ppermute(gram, axis, pairs)  9.9 us
    ppermute x4, waiting for transfers between devices, on_device(): gram = gram + lax.ppermute(gram, axis, pairs)  6.21 us
    ppermute x4, waiting for transfers between devices, pair_exchange(): lax.ppermute(first, axis, [p for a, b in firsts for p in ((a, b), (b, a))])  5.87 us
    pallas_call x1, Pallas kernels, on_device(): pl.pallas_call(functools.partial(assemble, nx, ny, two_z), out_shape=(pad...  4.22 us
    ppermute x1, starting transfers between devices, on_device(): other = lax.ppermute(gram, *stages[-1])  3.58 us
  transfers between devices with their start and end apart: 12, of which 8 were waited for; matrix products, arithmetic and copies ran while one was open for 0% of the time, Pallas kernels for 0%

profile of v1, /device:TPU:0, one launch (start us, length us, event | category | flops | bytes accessed | tf_op | source)
XLA Modules:
  0.0 95.1 jit_solution(7095316980412563914)
XLA Ops:
  0.6 1.9 %copy-done = f32[6,32,32,128]{3,2,1,0:T(8,128)S(1)} copy-done((f32[6,32,32,128]{3,2,1,0:T(8,128)S(1)}, f32[6,32,32,128]{3,2,1,0:T(8,128)}, u32[]{:S(2)}) %copy-start) | copy-done | bytes 3145752
  2.5 1.0 %copy-done.1 = f32[32,32,128]{2,1,0:T(8,128)S(1)} copy-done((f32[32,32,128]{2,1,0:T(8,128)S(1)}, f32[32,32,128]{2,1,0:T(8,128)}, u32[]{:S(2)}) %copy-start.1) | copy-done | bytes 524312
  4.1 0.6 collective-permute-start
  4.7 0.7 collective-permute-start.1
  5.3 2.6 %collective-permute-start.2 = (f32[672,128]{1,0:T(8,128)S(1)}, f32[672,128]{1,0:T(8,128)S(1)}, u32[]{:S(2)}, u32[]{:S(2)}) collective-permute-start(f32[672,128]{1,0:T(8,128)S(1)} %get-tuple-element.18), channel_id=1, source_target_pairs={{0,2},{2,0},{4,6},{6,4},{1,3},{3,1},{5,7},{7,5},{8,10},{10,8},{12,... | collective-permute-start | bytes 1032200 | tf_op jit(solution)/shard_map/ppermute | solution.py:34
  8.0 0.7 collective-permute-start.3
  8.7 4.4 %collective-permute-start.4 = (f32[128,128]{1,0:T(8,128)S(1)}, f32[128,128]{1,0:T(8,128)S(1)}, u32[]{:S(2)}, u32[]{:S(2)}) collective-permute-start(f32[128,128]{1,0:T(8,128)S(1)} %get-tuple-element.20), channel_id=1, source_target_pairs={{0,2},{2,0},{4,6},{6,4},{1,3},{3,1},{5,7},{7,5},{8,10},{10,8},{12,... | collective-permute-start | bytes 196616 | tf_op jit(solution)/shard_map/ppermute | solution.py:34
  13.2 0.7 collective-permute-start.5
  13.9 0.7 collective-permute-done.2.ya
  14.6 1.6 %collective-permute-done.4.ea = f32[128,128]{1,0:T(8,128)S(1)} collective-permute-done((f32[128,128]{1,0:T(8,128)S(1)}, f32[128,128]{1,0:T(8,128)S(1)}, u32[]{:S(2)}, u32[]{:S(2)}) %collective-permute-start.4) | collective-permute-done | bytes 65568 | tf_op jit(solution)/shard_map/ppermute | solution.py:34
  16.1 4.2 %assemble.1 = (f32[7,38,48,128]{3,2,1,0:T(8,128)S(1)}, f32[7,2,40,128]{3,2,1,0:T(8,128)S(1)}, f32[7,40,128]{2,1,0:T(8,128)S(1)}) custom-call(f32[7,38,48,128]{3,2,1,0:T(8,128)S(1)} %get-tuple-element.15.pad_in, f32[7,3,32,128]{3,2,1,0:T(8,128)S(1)} %collective-permute-done.xa_ref.xa, ...), custom_call_target="tpu_custom_call", output_to_operand_aliasing={{0}: (0, {})} | custom-call | tf_op jit(solution)/shard_map/assemble/pallas_call | solution.py:467
  20.4 2.3 %collective-permute-start.6 = (f32[7,40,128]{2,1,0:T(8,128)S(1)}, f32[7,40,128]{2,1,0:T(8,128)S(1)}, u32[]{:S(2)}, u32[]{:S(2)}) collective-permute-start(f32[7,40,128]{2,1,0:T(8,128)S(1)} %get-tuple-element.24), channel_id=1, source_target_pairs={{0,1},{1,0},{2,3},{3,2},{4,5},{5,4},{6,7},{7,6},{8,9},{9,8},{10,11... | collective-permute-start | bytes 430088 | tf_op jit(solution)/shard_map/ppermute | solution.py:34
  22.7 3.6 %collective-permute-done.6.za = f32[7,40,128]{2,1,0:T(8,128)S(1)} collective-permute-done((f32[7,40,128]{2,1,0:T(8,128)S(1)}, f32[7,40,128]{2,1,0:T(8,128)S(1)}, u32[]{:S(2)}, u32[]{:S(2)}) %collective-permute-start.6) | collective-permute-done | bytes 143392 | tf_op jit(solution)/shard_map/ppermute | solution.py:34
  26.2 27.8 %powers.1 = (bf16[128,192,128]{2,1,0:T(8,128)(2,1)S(1)}, bf16[128,192,128]{2,1,0:T(8,128)(2,1)S(1)}, f32[24,128]{1,0:T(8,128)S(1)}) custom-call(f32[7,38,48,128]{3,2,1,0:T(8,128)S(1)} %get-tuple-element.22.pad, f32[7,2,40,128]{3,2,1,0:T(8,128)S(1)} %get-tuple-element.23.own, f32[7,40,128]{2,1,0:T(8,128)S(1)} %collective-permute-done.6.za), custom_call_target="tpu_custom_call" | custom-call | tf_op jit(solution)/shard_map/powers/pallas_call | solution.py:481
  54.0 2.3 %collective-permute-start.7 = (f32[24,128]{1,0:T(8,128)S(1)}, f32[24,128]{1,0:T(8,128)S(1)}, u32[]{:S(2)}, u32[]{:S(2)}) collective-permute-start(f32[24,128]{1,0:T(8,128)S(1)} %get-tuple-element.25), channel_id=1, source_target_pairs={{0,1},{1,0},{2,3},{3,2},{4,5},{5,4},{6,7},{7,6},{8,9},{9,8},{10,11... | collective-permute-start | bytes 36872 | tf_op jit(solution)/shard_map/ppermute | solution.py:508
  56.3 1.7 %collective-permute-done.7 = f32[24,128]{1,0:T(8,128)S(1)} collective-permute-done((f32[24,128]{1,0:T(8,128)S(1)}, f32[24,128]{1,0:T(8,128)S(1)}, u32[]{:S(2)}, u32[]{:S(2)}) %collective-permute-start.7) | collective-permute-done | bytes 12320 | tf_op jit(solution)/shard_map/ppermute | solution.py:508
  58.0 1.2 %collective-permute-done.8 = f32[24,128]{1,0:T(8,128)S(1)} collective-permute-done((f32[24,128]{1,0:T(8,128)S(1)}, f32[24,128]{1,0:T(8,128)S(1)}, u32[]{:S(2)}, u32[]{:S(2)}) %collective-permute-start.8) | collective-permute-done | bytes 12320 | tf_op jit(solution)/shard_map/ppermute | solution.py:508
  59.2 3.0 %collective-permute-start.9 = (f32[24,128]{1,0:T(8,128)S(1)}, f32[24,128]{1,0:T(8,128)S(1)}, u32[]{:S(2)}, u32[]{:S(2)}) collective-permute-start(f32[24,128]{1,0:T(8,128)S(1)} %add.13), channel_id=1, source_target_pairs={{0,16},{8,24},{16,0},{24,8},{1,17},{9,25},{17,1},{25,9},{2,18},{10... | collective-permute-start | bytes 36872 | tf_op jit(solution)/shard_map/ppermute | solution.py:508
  62.2 1.7 %collective-permute-done.9 = f32[24,128]{1,0:T(8,128)S(1)} collective-permute-done((f32[24,128]{1,0:T(8,128)S(1)}, f32[24,128]{1,0:T(8,128)S(1)}, u32[]{:S(2)}, u32[]{:S(2)}) %collective-permute-start.9) | collective-permute-done | bytes 12320 | tf_op jit(solution)/shard_map/ppermute | solution.py:508
  63.9 4.6 %collective-permute-start.10 = (f32[24,128]{1,0:T(8,128)S(1)}, f32[24,128]{1,0:T(8,128)S(1)}, u32[]{:S(2)}, u32[]{:S(2)}) collective-permute-start(f32[24,128]{1,0:T(8,128)S(1)} %add.14), channel_id=1, source_target_pairs={{0,2},{2,0},{4,6},{6,4},{1,3},{3,1},{5,7},{7,5},{8,10},{10,8},{12,... | collective-permute-start | bytes 36872 | tf_op jit(solution)/shard_map/ppermute | solution.py:508
  68.5 1.7 %collective-permute-done.10 = f32[24,128]{1,0:T(8,128)S(1)} collective-permute-done((f32[24,128]{1,0:T(8,128)S(1)}, f32[24,128]{1,0:T(8,128)S(1)}, u32[]{:S(2)}, u32[]{:S(2)}) %collective-permute-start.10) | collective-permute-done | bytes 12320 | tf_op jit(solution)/shard_map/ppermute | solution.py:508
  70.2 3.6 %collective-permute-start.11 = (f32[24,128]{1,0:T(8,128)S(1)}, f32[24,128]{1,0:T(8,128)S(1)}, u32[]{:S(2)}, u32[]{:S(2)}) collective-permute-start(f32[24,128]{1,0:T(8,128)S(1)} %add.15.gram_a), channel_id=1, source_target_pairs={{0,4},{2,6},{4,0},{6,2},{1,5},{3,7},{5,1},{7,3},{8,12},{10,14},{12... | collective-permute-start | bytes 36872 | tf_op jit(solution)/shard_map/ppermute | solution.py:509
  73.8 1.7 %collective-permute-done.11.gram_b = f32[24,128]{1,0:T(8,128)S(1)} collective-permute-done((f32[24,128]{1,0:T(8,128)S(1)}, f32[24,128]{1,0:T(8,128)S(1)}, u32[]{:S(2)}, u32[]{:S(2)}) %collective-permute-start.11) | collective-permute-done | bytes 12320 | tf_op jit(solution)/shard_map/ppermute | solution.py:509
  75.4 19.6 %factor_and_solve.1 = (f32[24,32,32,128]{3,2,1,0:T(8,128)}, f32[24,24]{1,0:T(8,128)}) custom-call(f32[24,128]{1,0:T(8,128)S(1)} %add.15.gram_a, f32[24,128]{1,0:T(8,128)S(1)} %collective-permute-done.11.gram_b, bf16[128,192,128]{2,1,0:T(8,128)(2,1)S(1)} %get-tuple-element.26.high_ref, bf16[128,192,128]{2,1,0:T(8,128)(2,1)S(1)} %get-tuple-element.27.low_ref), custom_call_target="tpu_custom_call" | custom-call | tf_op jit(solution)/shard_map/factor_and_solve/pallas_call | solution.py:511
  (13 shorter events, 0.6 us)
Async XLA Ops:
  0.6 1.9 %copy-start = (f32[6,32,32,128]{3,2,1,0:T(8,128)S(1)}, f32[6,32,32,128]{3,2,1,0:T(8,128)}, u32[]{:S(2)}) copy-start(f32[6,32,32,128]{3,2,1,0:T(8,128)} %rs_ref.1) | copy-start | bytes 9437188
  2.5 1.0 %copy-start.1 = (f32[32,32,128]{2,1,0:T(8,128)S(1)}, f32[32,32,128]{2,1,0:T(8,128)}, u32[]{:S(2)}) copy-start(f32[32,32,128]{2,1,0:T(8,128)} %k_ref.1) | copy-start | bytes 1572868
  4.1 4.6 %collective-permute-start = (f32[7,3,32,128]{3,2,1,0:T(8,128)S(1)}, f32[7,3,32,128]{3,2,1,0:T(8,128)S(1)}, u32[]{:S(2)}, u32[]{:S(2)}) collective-permute-start(f32[7,3,32,128]{3,2,1,0:T(8,128)S(1)} %get-tuple-element.16), channel_id=1, source_target_pairs={{0,8},{8,0},{16,24},{24,16},{1,9},{9,1},{17,25},{25,17},{2,10},{10... | collective-permute-start | bytes 1032200 | tf_op jit(solution)/shard_map/ppermute | solution.py:34
  4.7 4.0 %collective-permute-start.1 = (f32[7,3,32,128]{3,2,1,0:T(8,128)S(1)}, f32[7,3,32,128]{3,2,1,0:T(8,128)S(1)}, u32[]{:S(2)}, u32[]{:S(2)}) collective-permute-start(f32[7,3,32,128]{3,2,1,0:T(8,128)S(1)} %get-tuple-element.17), channel_id=1, source_target_pairs={{8,16},{16,8},{9,17},{17,9},{10,18},{18,10},{11,19},{19,11},{12,20... | collective-permute-start | bytes 1032200 | tf_op jit(solution)/shard_map/ppermute | solution.py:37
  5.3 9.2 %collective-permute-start.2 = (f32[672,128]{1,0:T(8,128)S(1)}, f32[672,128]{1,0:T(8,128)S(1)}, u32[]{:S(2)}, u32[]{:S(2)}) collective-permute-start(f32[672,128]{1,0:T(8,128)S(1)} %get-tuple-element.18), channel_id=1, source_target_pairs={{0,2},{2,0},{4,6},{6,4},{1,3},{3,1},{5,7},{7,5},{8,10},{10,8},{12,... | collective-permute-start | bytes 1032200 | tf_op jit(solution)/shard_map/ppermute | solution.py:34
  8.0 6.6 %collective-permute-start.3 = (f32[672,128]{1,0:T(8,128)S(1)}, f32[672,128]{1,0:T(8,128)S(1)}, u32[]{:S(2)}, u32[]{:S(2)}) collective-permute-start(f32[672,128]{1,0:T(8,128)S(1)} %get-tuple-element.19), channel_id=1, source_target_pairs={{2,4},{4,2},{3,5},{5,3},{10,12},{12,10},{11,13},{13,11},{18,20},{2... | collective-permute-start | bytes 1032200 | tf_op jit(solution)/shard_map/ppermute | solution.py:37
  8.7 7.4 %collective-permute-start.4 = (f32[128,128]{1,0:T(8,128)S(1)}, f32[128,128]{1,0:T(8,128)S(1)}, u32[]{:S(2)}, u32[]{:S(2)}) collective-permute-start(f32[128,128]{1,0:T(8,128)S(1)} %get-tuple-element.20), channel_id=1, source_target_pairs={{0,2},{2,0},{4,6},{6,4},{1,3},{3,1},{5,7},{7,5},{8,10},{10,8},{12,... | collective-permute-start | bytes 196616 | tf_op jit(solution)/shard_map/ppermute | solution.py:34
  13.2 2.9 %collective-permute-start.5 = (f32[128,128]{1,0:T(8,128)S(1)}, f32[128,128]{1,0:T(8,128)S(1)}, u32[]{:S(2)}, u32[]{:S(2)}) collective-permute-start(f32[128,128]{1,0:T(8,128)S(1)} %get-tuple-element.21), channel_id=1, source_target_pairs={{2,4},{4,2},{3,5},{5,3},{10,12},{12,10},{11,13},{13,11},{18,20},{2... | collective-permute-start | bytes 196616 | tf_op jit(solution)/shard_map/ppermute | solution.py:37
  20.4 5.9 %collective-permute-start.6 = (f32[7,40,128]{2,1,0:T(8,128)S(1)}, f32[7,40,128]{2,1,0:T(8,128)S(1)}, u32[]{:S(2)}, u32[]{:S(2)}) collective-permute-start(f32[7,40,128]{2,1,0:T(8,128)S(1)} %get-tuple-element.24), channel_id=1, source_target_pairs={{0,1},{1,0},{2,3},{3,2},{4,5},{5,4},{6,7},{7,6},{8,9},{9,8},{10,11... | collective-permute-start | bytes 430088 | tf_op jit(solution)/shard_map/ppermute | solution.py:34
  54.0 4.0 %collective-permute-start.7 = (f32[24,128]{1,0:T(8,128)S(1)}, f32[24,128]{1,0:T(8,128)S(1)}, u32[]{:S(2)}, u32[]{:S(2)}) collective-permute-start(f32[24,128]{1,0:T(8,128)S(1)} %get-tuple-element.25), channel_id=1, source_target_pairs={{0,1},{1,0},{2,3},{3,2},{4,5},{5,4},{6,7},{7,6},{8,9},{9,8},{10,11... | collective-permute-start | bytes 36872 | tf_op jit(solution)/shard_map/ppermute | solution.py:508
  58.0 1.2 %collective-permute-start.8 = (f32[24,128]{1,0:T(8,128)S(1)}, f32[24,128]{1,0:T(8,128)S(1)}, u32[]{:S(2)}, u32[]{:S(2)}) collective-permute-start(f32[24,128]{1,0:T(8,128)S(1)} %add.12), channel_id=1, source_target_pairs={{0,8},{8,0},{16,24},{24,16},{1,9},{9,1},{17,25},{25,17},{2,10},{10... | collective-permute-start | bytes 36872 | tf_op jit(solution)/shard_map/ppermute | solution.py:508
  59.2 4.7 %collective-permute-start.9 = (f32[24,128]{1,0:T(8,128)S(1)}, f32[24,128]{1,0:T(8,128)S(1)}, u32[]{:S(2)}, u32[]{:S(2)}) collective-permute-start(f32[24,128]{1,0:T(8,128)S(1)} %add.13), channel_id=1, source_target_pairs={{0,16},{8,24},{16,0},{24,8},{1,17},{9,25},{17,1},{25,9},{2,18},{10... | collective-permute-start | bytes 36872 | tf_op jit(solution)/shard_map/ppermute | solution.py:508
  63.9 6.3 %collective-permute-start.10 = (f32[24,128]{1,0:T(8,128)S(1)}, f32[24,128]{1,0:T(8,128)S(1)}, u32[]{:S(2)}, u32[]{:S(2)}) collective-permute-start(f32[24,128]{1,0:T(8,128)S(1)} %add.14), channel_id=1, source_target_pairs={{0,2},{2,0},{4,6},{6,4},{1,3},{3,1},{5,7},{7,5},{8,10},{10,8},{12,... | collective-permute-start | bytes 36872 | tf_op jit(solution)/shard_map/ppermute | solution.py:508
  70.2 5.2 %collective-permute-start.11 = (f32[24,128]{1,0:T(8,128)S(1)}, f32[24,128]{1,0:T(8,128)S(1)}, u32[]{:S(2)}, u32[]{:S(2)}) collective-permute-start(f32[24,128]{1,0:T(8,128)S(1)} %add.15.gram_a), channel_id=1, source_target_pairs={{0,4},{2,6},{4,0},{6,2},{1,5},{3,7},{5,1},{7,3},{8,12},{10,14},{12... | collective-permute-start | bytes 36872 | tf_op jit(solution)/shard_map/ppermute | solution.py:509

commit v2 on v1

--- a/solution.py
+++ b/solution.py
@@ -13,6 +13,7 @@
 LANES = 128
 TOP = 8
 MIB = 1 << 20
+TOGETHER = 2
 
 
 def even_on(axis):
@@ -282,8 +283,7 @@
     def weights_at(plane, y):
         return [coef[n, plane - 1, y + 2 : y + 10, :] for n in range(6)]
 
-    @pl.loop(1, nx + 5)
-    def _(plane):
+    def first_power(plane):
         for t in range(tiles):
             y = 8 * t - 2
             weights = weights_at(plane, y)
@@ -293,8 +293,7 @@
                     pad, 0, edge, f, plane, y, weights
                 )
 
-    @pl.loop(2, nx + 4)
-    def _(plane):
+    def second_power(plane):
         for t in range(tiles):
             y = 8 * t - 1
             weights = weights_at(plane, y)
@@ -334,14 +333,33 @@
         )
 
     acc[...] = jnp.zeros_like(acc)
-    last_power(DEPTH)
-
-    @pl.loop(DEPTH + 1, nx + DEPTH)
+
+    @pl.loop(1, 4)
     def _(plane):
-        last_power(plane)
-        products(plane - 1)
-
-    products(nx + DEPTH - 1)
+        first_power(plane)
+
+    @pl.loop(4, 7)
+    def _(plane):
+        second_power(plane - 2)
+        first_power(plane)
+
+    last_power(3)
+    second_power(5)
+    first_power(7)
+
+    @pl.loop(8, nx + 5)
+    def _(plane):
+        products(plane - 5)
+        last_power(plane - 4)
+        second_power(plane - 2)
+        first_power(plane)
+
+    products(nx)
+    last_power(nx + 1)
+    second_power(nx + 3)
+    products(nx + 1)
+    last_power(nx + 2)
+    products(nx + 2)
 
     rows = acc.shape[1]
     sums = acc[...]
@@ -360,60 +378,75 @@
     gram_ref[...] = small[0:order, :] + cross + square[...].T[0:order, :]
 
 
-def factor_and_solve(cells, order, ny, gram_a, gram_b, high_ref, low_ref, out_ref, factor_ref, w_wide, w_low):
+def factor_and_solve(
+    cells, order, nx, ny, gram_a, gram_b, high_ref, low_ref, out_ref, factor_ref, w_wide, w_low, held, sem
+):
     blocks = ny // 8
     rows = 8 * order
 
-    @pl.when(pl.program_id(0) == 0)
-    def _():
-        row = lax.broadcasted_iota(jnp.int32, (order, LANES), 0)
-        lane = lax.broadcasted_iota(jnp.int32, (order, LANES), 1)
-        work = (gram_a[...] + gram_b[...]) / cells
-        work = jnp.where(lane < order, work, jnp.where(lane == row + 64, 1.0, 0.0))
-        for j in range(order):
-            pivot = work[j : j + 1, :]
-            factor = work[:, j : j + 1] / work[j : j + 1, j : j + 1]
-            work = work - jnp.where(row > j, factor * pivot, 0.0)
-        pivots = jnp.sum(jnp.where(lane == row, work, 0.0), 1, keepdims=True)
-        work = work / jnp.sqrt(pivots)
-        factor_ref[...] = jnp.where(lane >= row, work, 0.0)[:, :order]
-        inverse = pltpu.roll(work, 64, 1)
-        inverse = jnp.where(lane <= row, inverse, 0.0)
-        high = inverse.astype(BF16)
-        low = (inverse - high.astype(F32)).astype(BF16)
-        spread = (
-            lax.broadcasted_iota(jnp.int32, (rows, order), 0) // 8
-            == lax.broadcasted_iota(jnp.int32, (rows, order), 1)
-        ).astype(BF16)
-        across = (
-            lax.broadcasted_iota(jnp.int32, (LANES, rows), 1) // 8
-            == lax.broadcasted_iota(jnp.int32, (LANES, rows), 0)
-        ).astype(BF16)
-        same = lax.broadcasted_iota(jnp.int32, (rows, rows), 0) % 8 == (
-            lax.broadcasted_iota(jnp.int32, (rows, rows), 1) % 8
-        )
-
-        def kron(small):
-            tall = jnp.dot(spread, small, preferred_element_type=F32).astype(BF16)
-            full = jnp.dot(tall, across, preferred_element_type=F32)
-            return jnp.where(same, full, 0.0).astype(BF16)
-
-        w_high = kron(high)
-        w_wide[:, :rows] = w_high
-        w_wide[:, rows:] = w_high
-        w_low[...] = kron(low)
-
-    base = pl.program_id(0) * blocks
-    high = jnp.concatenate([high_ref[base + t] for t in range(blocks)], 1)
-    low = jnp.concatenate([low_ref[base + t] for t in range(blocks)], 1)
-    both = jnp.concatenate([high, low], 0)
-    result = jnp.dot(w_wide[...], both, preferred_element_type=F32)
-    result = result + jnp.dot(w_low[...], high, preferred_element_type=F32)
-    for t in range(blocks):
-        for b in range(order):
-            out_ref[b, 0, 8 * t : 8 * t + 8, :] = result[
-                8 * b : 8 * b + 8, LANES * t : LANES * t + LANES
-            ]
+    row = lax.broadcasted_iota(jnp.int32, (order, LANES), 0)
+    lane = lax.broadcasted_iota(jnp.int32, (order, LANES), 1)
+    work = (gram_a[...] + gram_b[...]) / cells
+    work = jnp.where(lane < order, work, jnp.where(lane == row + 64, 1.0, 0.0))
+    for j in range(order):
+        pivot = work[j : j + 1, :]
+        factor = work[:, j : j + 1] / work[j : j + 1, j : j + 1]
+        work = work - jnp.where(row > j, factor * pivot, 0.0)
+    pivots = jnp.sum(jnp.where(lane == row, work, 0.0), 1, keepdims=True)
+    work = work / jnp.sqrt(pivots)
+    factor_ref[...] = jnp.where(lane >= row, work, 0.0)[:, :order]
+    inverse = pltpu.roll(work, 64, 1)
+    inverse = jnp.where(lane <= row, inverse, 0.0)
+    high = inverse.astype(BF16)
+    low = (inverse - high.astype(F32)).astype(BF16)
+    spread = (
+        lax.broadcasted_iota(jnp.int32, (rows, order), 0) // 8
+        == lax.broadcasted_iota(jnp.int32, (rows, order), 1)
+    ).astype(BF16)
+    across = (
+        lax.broadcasted_iota(jnp.int32, (LANES, rows), 1) // 8
+        == lax.broadcasted_iota(jnp.int32, (LANES, rows), 0)
+    ).astype(BF16)
+    same = lax.broadcasted_iota(jnp.int32, (rows, rows), 0) % 8 == (
+        lax.broadcasted_iota(jnp.int32, (rows, rows), 1) % 8
+    )
+
+    def kron(small):
+        tall = jnp.dot(spread, small, preferred_element_type=F32).astype(BF16)
+        full = jnp.dot(tall, across, preferred_element_type=F32)
+        return jnp.where(same, full, 0.0).astype(BF16)
+
+    w_high = kron(high)
+    w_wide[:, :rows] = w_high
+    w_wide[:, rows:] = w_high
+    w_low[...] = kron(low)
+
+    def solve(plane):
+        base = plane * blocks
+        high = jnp.concatenate([high_ref[base + t] for t in range(blocks)], 1)
+        low = jnp.concatenate([low_ref[base + t] for t in range(blocks)], 1)
+        both = jnp.concatenate([high, low], 0)
+        result = jnp.dot(w_wide[...], both, preferred_element_type=F32)
+        result = result + jnp.dot(w_low[...], high, preferred_element_type=F32)
+        for t in range(blocks):
+            for b in range(order):
+                held[b, plane, 8 * t : 8 * t + 8, :] = result[
+                    8 * b : 8 * b + 8, LANES * t : LANES * t + LANES
+                ]
+
+    def store(step):
+        part = pl.ds(step * TOGETHER, TOGETHER)
+        return pltpu.make_async_copy(held.at[:, part], out_ref.at[:, part], sem.at[step])
+
+    @pl.loop(0, nx // TOGETHER)
+    def _(step):
+        for u in range(TOGETHER):
+            solve(step * TOGETHER + u)
+        store(step).start()
+
+    @pl.loop(0, nx // TOGETHER)
+    def _(step):
+        store(step).wait()
 
 
 VM = functools.partial(pl.BlockSpec, memory_space=pltpu.VMEM)
@@ -443,7 +476,7 @@
     pad, xa, xb, ya, yb = pl.pallas_call(
         pack_faces,
         out_shape=(pad_type, x_type, x_type, y_type, y_type),
-        in_specs=[pl.BlockSpec(memory_space=pl.ANY)] * 2,
+        in_specs=[pl.BlockSpec(memory_space=pltpu.HBM)] * 2,
         out_specs=(VM(),) * 5,
         scratch_shapes=[pltpu.SemaphoreType.DMA((slabs,))],
         compiler_params=params(8),
@@ -509,19 +542,20 @@
     other = lax.ppermute(gram, *stages[-1])
 
     basis_q, factor_r = pl.pallas_call(
-        functools.partial(factor_and_solve, cells, order, ny),
-        grid=(nx,),
+        functools.partial(factor_and_solve, cells, order, nx, ny),
         out_shape=(
             jax.ShapeDtypeStruct((order, nx, ny, nz), F32),
             jax.ShapeDtypeStruct((order, order), F32),
         ),
         in_specs=[VM()] * 4,
-        out_specs=(
-            pl.BlockSpec((order, 1, ny, nz), lambda i: (0, i, 0, 0)),
-            pl.BlockSpec((order, order), lambda i: (0, 0)),
-        ),
-        scratch_shapes=[pltpu.VMEM((rows, 2 * rows), BF16), pltpu.VMEM((rows, rows), BF16)],
-        compiler_params=params(16),
+        out_specs=(pl.BlockSpec(memory_space=pltpu.HBM), VM()),
+        scratch_shapes=[
+            pltpu.VMEM((rows, 2 * rows), BF16),
+            pltpu.VMEM((rows, rows), BF16),
+            pltpu.VMEM((order, nx, ny, nz), F32),
+            pltpu.SemaphoreType.DMA((nx // TOGETHER,)),
+        ],
+        compiler_params=params(24),
         name="factor_and_solve",
     )(gram, other, high, low)
     return (basis_q, factor_r)

time: 95.3 us -> 79.1 us (0.83)
  Pallas kernels: 52.2 us -> 36 us
    pallas_call x1, Pallas kernels: 19.6 us -> 11.5 us  [on_device(): pl.pallas_call(functools.partial(factor_and_solve, cells, order, nx, ny),...]
    pallas_call x1, Pallas kernels: 27.8 us -> 19.7 us  [on_device(): pl.pallas_call(functools.partial(powers, nx, ny, two_z), out_shape=(split...]
where the time goes in v2:
time: 79.1 us; the launch traced here: 78.8 us
  Pallas kernels  36 us (46%)
  starting transfers between devices  25.4 us (32%)
  waiting for transfers between devices  13.8 us (17%)
  local copies, waits for them, and re-layouts  2.92 us (4%)
    pallas_call x1, Pallas kernels, on_device(): pl.pallas_call(functools.partial(powers, nx, ny, two_z), out_shape=(split...  19.7 us
    pallas_call x1, Pallas kernels, on_device(): pl.pallas_call(functools.partial(factor_and_solve, cells, order, nx, ny),...  11.5 us
    ppermute x4, starting transfers between devices, pair_exchange(): lax.ppermute(first, axis, [p for a, b in firsts for p in ((a, b), (b, a))])  9.94 us
    ppermute x4, starting transfers between devices, on_device(): gram = gram + lax.ppermute(gram, axis, pairs)  9.91 us
    ppermute x4, waiting for transfers between devices, on_device(): gram = gram + lax.ppermute(gram, axis, pairs)  6.2 us
    ppermute x4, waiting for transfers between devices, pair_exchange(): lax.ppermute(first, axis, [p for a, b in firsts for p in ((a, b), (b, a))])  5.87 us
    pallas_call x1, Pallas kernels, on_device(): pl.pallas_call(functools.partial(assemble, nx, ny, two_z), out_shape=(pad...  4.22 us
    ppermute x1, starting transfers between devices, on_device(): other = lax.ppermute(gram, *stages[-1])  3.58 us
  transfers between devices with their start and end apart: 12, of which 8 were waited for; matrix products, arithmetic and copies ran while one was open for 0% of the time, Pallas kernels for 0%

profile of v2, /device:TPU:0, one launch (start us, length us, event | category | flops | bytes accessed | tf_op | source)
XLA Modules:
  0.0 78.8 jit_solution(17539620767597892178)
XLA Ops:
  0.6 1.9 %copy-done = f32[6,32,32,128]{3,2,1,0:T(8,128)S(1)} copy-done((f32[6,32,32,128]{3,2,1,0:T(8,128)S(1)}, f32[6,32,32,128]{3,2,1,0:T(8,128)}, u32[]{:S(2)}) %copy-start) | copy-done | bytes 3145752
  2.5 1.0 %copy-done.1 = f32[32,32,128]{2,1,0:T(8,128)S(1)} copy-done((f32[32,32,128]{2,1,0:T(8,128)S(1)}, f32[32,32,128]{2,1,0:T(8,128)}, u32[]{:S(2)}) %copy-start.1) | copy-done | bytes 524312
  4.1 0.6 collective-permute-start
  4.7 0.7 collective-permute-start.1
  5.3 2.6 %collective-permute-start.2 = (f32[672,128]{1,0:T(8,128)S(1)}, f32[672,128]{1,0:T(8,128)S(1)}, u32[]{:S(2)}, u32[]{:S(2)}) collective-permute-start(f32[672,128]{1,0:T(8,128)S(1)} %get-tuple-element.18), channel_id=1, source_target_pairs={{0,2},{2,0},{4,6},{6,4},{1,3},{3,1},{5,7},{7,5},{8,10},{10,8},{12,... | collective-permute-start | bytes 1032200 | tf_op jit(solution)/shard_map/ppermute | solution.py:35
  8.0 0.7 collective-permute-start.3
  8.7 4.4 %collective-permute-start.4 = (f32[128,128]{1,0:T(8,128)S(1)}, f32[128,128]{1,0:T(8,128)S(1)}, u32[]{:S(2)}, u32[]{:S(2)}) collective-permute-start(f32[128,128]{1,0:T(8,128)S(1)} %get-tuple-element.20), channel_id=1, source_target_pairs={{0,2},{2,0},{4,6},{6,4},{1,3},{3,1},{5,7},{7,5},{8,10},{10,8},{12,... | collective-permute-start | bytes 196616 | tf_op jit(solution)/shard_map/ppermute | solution.py:35
  13.2 0.7 collective-permute-start.5
  13.9 0.7 collective-permute-done.2.ya
  14.6 1.6 %collective-permute-done.4.ea = f32[128,128]{1,0:T(8,128)S(1)} collective-permute-done((f32[128,128]{1,0:T(8,128)S(1)}, f32[128,128]{1,0:T(8,128)S(1)}, u32[]{:S(2)}, u32[]{:S(2)}) %collective-permute-start.4) | collective-permute-done | bytes 65568 | tf_op jit(solution)/shard_map/ppermute | solution.py:35
  16.1 4.2 %assemble.1 = (f32[7,38,48,128]{3,2,1,0:T(8,128)S(1)}, f32[7,2,40,128]{3,2,1,0:T(8,128)S(1)}, f32[7,40,128]{2,1,0:T(8,128)S(1)}) custom-call(f32[7,38,48,128]{3,2,1,0:T(8,128)S(1)} %get-tuple-element.15.pad_in, f32[7,3,32,128]{3,2,1,0:T(8,128)S(1)} %collective-permute-done.xa_ref.xa, ...), custom_call_target="tpu_custom_call", output_to_operand_aliasing={{0}: (0, {})} | custom-call | tf_op jit(solution)/shard_map/assemble/pallas_call | solution.py:500
  20.4 2.3 %collective-permute-start.6 = (f32[7,40,128]{2,1,0:T(8,128)S(1)}, f32[7,40,128]{2,1,0:T(8,128)S(1)}, u32[]{:S(2)}, u32[]{:S(2)}) collective-permute-start(f32[7,40,128]{2,1,0:T(8,128)S(1)} %get-tuple-element.24), channel_id=1, source_target_pairs={{0,1},{1,0},{2,3},{3,2},{4,5},{5,4},{6,7},{7,6},{8,9},{9,8},{10,11... | collective-permute-start | bytes 430088 | tf_op jit(solution)/shard_map/ppermute | solution.py:35
  22.7 3.6 %collective-permute-done.6.za = f32[7,40,128]{2,1,0:T(8,128)S(1)} collective-permute-done((f32[7,40,128]{2,1,0:T(8,128)S(1)}, f32[7,40,128]{2,1,0:T(8,128)S(1)}, u32[]{:S(2)}, u32[]{:S(2)}) %collective-permute-start.6) | collective-permute-done | bytes 143392 | tf_op jit(solution)/shard_map/ppermute | solution.py:35
  26.2 19.7 %powers.1 = (bf16[128,192,128]{2,1,0:T(8,128)(2,1)S(1)}, bf16[128,192,128]{2,1,0:T(8,128)(2,1)S(1)}, f32[24,128]{1,0:T(8,128)S(1)}) custom-call(f32[7,38,48,128]{3,2,1,0:T(8,128)S(1)} %get-tuple-element.22.pad, f32[7,2,40,128]{3,2,1,0:T(8,128)S(1)} %get-tuple-element.23.own, f32[7,40,128]{2,1,0:T(8,128)S(1)} %collective-permute-done.6.za), custom_call_target="tpu_custom_call" | custom-call | tf_op jit(solution)/shard_map/powers/pallas_call | solution.py:514
  45.9 2.3 %collective-permute-start.7 = (f32[24,128]{1,0:T(8,128)S(1)}, f32[24,128]{1,0:T(8,128)S(1)}, u32[]{:S(2)}, u32[]{:S(2)}) collective-permute-start(f32[24,128]{1,0:T(8,128)S(1)} %get-tuple-element.25), channel_id=1, source_target_pairs={{0,1},{1,0},{2,3},{3,2},{4,5},{5,4},{6,7},{7,6},{8,9},{9,8},{10,11... | collective-permute-start | bytes 36872 | tf_op jit(solution)/shard_map/ppermute | solution.py:541
  48.3 1.7 %collective-permute-done.7 = f32[24,128]{1,0:T(8,128)S(1)} collective-permute-done((f32[24,128]{1,0:T(8,128)S(1)}, f32[24,128]{1,0:T(8,128)S(1)}, u32[]{:S(2)}, u32[]{:S(2)}) %collective-permute-start.7) | collective-permute-done | bytes 12320 | tf_op jit(solution)/shard_map/ppermute | solution.py:541
  49.9 1.2 %collective-permute-done.8 = f32[24,128]{1,0:T(8,128)S(1)} collective-permute-done((f32[24,128]{1,0:T(8,128)S(1)}, f32[24,128]{1,0:T(8,128)S(1)}, u32[]{:S(2)}, u32[]{:S(2)}) %collective-permute-start.8) | collective-permute-done | bytes 12320 | tf_op jit(solution)/shard_map/ppermute | solution.py:541
  51.1 3.0 %collective-permute-start.9 = (f32[24,128]{1,0:T(8,128)S(1)}, f32[24,128]{1,0:T(8,128)S(1)}, u32[]{:S(2)}, u32[]{:S(2)}) collective-permute-start(f32[24,128]{1,0:T(8,128)S(1)} %add.13), channel_id=1, source_target_pairs={{0,16},{8,24},{16,0},{24,8},{1,17},{9,25},{17,1},{25,9},{2,18},{10... | collective-permute-start | bytes 36872 | tf_op jit(solution)/shard_map/ppermute | solution.py:541
  54.1 1.7 %collective-permute-done.9 = f32[24,128]{1,0:T(8,128)S(1)} collective-permute-done((f32[24,128]{1,0:T(8,128)S(1)}, f32[24,128]{1,0:T(8,128)S(1)}, u32[]{:S(2)}, u32[]{:S(2)}) %collective-permute-start.9) | collective-permute-done | bytes 12320 | tf_op jit(solution)/shard_map/ppermute | solution.py:541
  55.8 4.6 %collective-permute-start.10 = (f32[24,128]{1,0:T(8,128)S(1)}, f32[24,128]{1,0:T(8,128)S(1)}, u32[]{:S(2)}, u32[]{:S(2)}) collective-permute-start(f32[24,128]{1,0:T(8,128)S(1)} %add.14), channel_id=1, source_target_pairs={{0,2},{2,0},{4,6},{6,4},{1,3},{3,1},{5,7},{7,5},{8,10},{10,8},{12,... | collective-permute-start | bytes 36872 | tf_op jit(solution)/shard_map/ppermute | solution.py:541
  60.4 1.7 %collective-permute-done.10 = f32[24,128]{1,0:T(8,128)S(1)} collective-permute-done((f32[24,128]{1,0:T(8,128)S(1)}, f32[24,128]{1,0:T(8,128)S(1)}, u32[]{:S(2)}, u32[]{:S(2)}) %collective-permute-start.10) | collective-permute-done | bytes 12320 | tf_op jit(solution)/shard_map/ppermute | solution.py:541
  62.1 3.6 %collective-permute-start.11 = (f32[24,128]{1,0:T(8,128)S(1)}, f32[24,128]{1,0:T(8,128)S(1)}, u32[]{:S(2)}, u32[]{:S(2)}) collective-permute-start(f32[24,128]{1,0:T(8,128)S(1)} %add.15.gram_a), channel_id=1, source_target_pairs={{0,4},{2,6},{4,0},{6,2},{1,5},{3,7},{5,1},{7,3},{8,12},{10,14},{12... | collective-permute-start | bytes 36872 | tf_op jit(solution)/shard_map/ppermute | solution.py:542
  65.6 1.7 %collective-permute-done.11.gram_b = f32[24,128]{1,0:T(8,128)S(1)} collective-permute-done((f32[24,128]{1,0:T(8,128)S(1)}, f32[24,128]{1,0:T(8,128)S(1)}, u32[]{:S(2)}, u32[]{:S(2)}) %collective-permute-start.11) | collective-permute-done | bytes 12320 | tf_op jit(solution)/shard_map/ppermute | solution.py:542
  67.3 11.5 %factor_and_solve.1 = (f32[24,32,32,128]{3,2,1,0:T(8,128)}, f32[24,24]{1,0:T(8,128)}) custom-call(f32[24,128]{1,0:T(8,128)S(1)} %add.15.gram_a, f32[24,128]{1,0:T(8,128)S(1)} %collective-permute-done.11.gram_b, bf16[128,192,128]{2,1,0:T(8,128)(2,1)S(1)} %get-tuple-element.26.high_ref, bf16[128,192,128]{2,1,0:T(8,128)(2,1)S(1)} %get-tuple-element.27.low_ref), custom_call_target="tpu_custom_call" | custom-call | tf_op jit(solution)/shard_map/factor_and_solve/pallas_call | solution.py:544
  (13 shorter events, 0.6 us)
Async XLA Ops:
  0.6 1.9 %copy-start = (f32[6,32,32,128]{3,2,1,0:T(8,128)S(1)}, f32[6,32,32,128]{3,2,1,0:T(8,128)}, u32[]{:S(2)}) copy-start(f32[6,32,32,128]{3,2,1,0:T(8,128)} %rs_ref.1) | copy-start | bytes 9437188
  2.5 1.0 %copy-start.1 = (f32[32,32,128]{2,1,0:T(8,128)S(1)}, f32[32,32,128]{2,1,0:T(8,128)}, u32[]{:S(2)}) copy-start(f32[32,32,128]{2,1,0:T(8,128)} %k_ref.1) | copy-start | bytes 1572868
  4.1 4.6 %collective-permute-start = (f32[7,3,32,128]{3,2,1,0:T(8,128)S(1)}, f32[7,3,32,128]{3,2,1,0:T(8,128)S(1)}, u32[]{:S(2)}, u32[]{:S(2)}) collective-permute-start(f32[7,3,32,128]{3,2,1,0:T(8,128)S(1)} %get-tuple-element.16), channel_id=1, source_target_pairs={{0,8},{8,0},{16,24},{24,16},{1,9},{9,1},{17,25},{25,17},{2,10},{10... | collective-permute-start | bytes 1032200 | tf_op jit(solution)/shard_map/ppermute | solution.py:35
  4.7 4.0 %collective-permute-start.1 = (f32[7,3,32,128]{3,2,1,0:T(8,128)S(1)}, f32[7,3,32,128]{3,2,1,0:T(8,128)S(1)}, u32[]{:S(2)}, u32[]{:S(2)}) collective-permute-start(f32[7,3,32,128]{3,2,1,0:T(8,128)S(1)} %get-tuple-element.17), channel_id=1, source_target_pairs={{8,16},{16,8},{9,17},{17,9},{10,18},{18,10},{11,19},{19,11},{12,20... | collective-permute-start | bytes 1032200 | tf_op jit(solution)/shard_map/ppermute | solution.py:38
  5.3 9.2 %collective-permute-start.2 = (f32[672,128]{1,0:T(8,128)S(1)}, f32[672,128]{1,0:T(8,128)S(1)}, u32[]{:S(2)}, u32[]{:S(2)}) collective-permute-start(f32[672,128]{1,0:T(8,128)S(1)} %get-tuple-element.18), channel_id=1, source_target_pairs={{0,2},{2,0},{4,6},{6,4},{1,3},{3,1},{5,7},{7,5},{8,10},{10,8},{12,... | collective-permute-start | bytes 1032200 | tf_op jit(solution)/shard_map/ppermute | solution.py:35
  8.0 6.6 %collective-permute-start.3 = (f32[672,128]{1,0:T(8,128)S(1)}, f32[672,128]{1,0:T(8,128)S(1)}, u32[]{:S(2)}, u32[]{:S(2)}) collective-permute-start(f32[672,128]{1,0:T(8,128)S(1)} %get-tuple-element.19), channel_id=1, source_target_pairs={{2,4},{4,2},{3,5},{5,3},{10,12},{12,10},{11,13},{13,11},{18,20},{2... | collective-permute-start | bytes 1032200 | tf_op jit(solution)/shard_map/ppermute | solution.py:38
  8.7 7.4 %collective-permute-start.4 = (f32[128,128]{1,0:T(8,128)S(1)}, f32[128,128]{1,0:T(8,128)S(1)}, u32[]{:S(2)}, u32[]{:S(2)}) collective-permute-start(f32[128,128]{1,0:T(8,128)S(1)} %get-tuple-element.20), channel_id=1, source_target_pairs={{0,2},{2,0},{4,6},{6,4},{1,3},{3,1},{5,7},{7,5},{8,10},{10,8},{12,... | collective-permute-start | bytes 196616 | tf_op jit(solution)/shard_map/ppermute | solution.py:35
  13.2 2.9 %collective-permute-start.5 = (f32[128,128]{1,0:T(8,128)S(1)}, f32[128,128]{1,0:T(8,128)S(1)}, u32[]{:S(2)}, u32[]{:S(2)}) collective-permute-start(f32[128,128]{1,0:T(8,128)S(1)} %get-tuple-element.21), channel_id=1, source_target_pairs={{2,4},{4,2},{3,5},{5,3},{10,12},{12,10},{11,13},{13,11},{18,20},{2... | collective-permute-start | bytes 196616 | tf_op jit(solution)/shard_map/ppermute | solution.py:38
  20.4 5.9 %collective-permute-start.6 = (f32[7,40,128]{2,1,0:T(8,128)S(1)}, f32[7,40,128]{2,1,0:T(8,128)S(1)}, u32[]{:S(2)}, u32[]{:S(2)}) collective-permute-start(f32[7,40,128]{2,1,0:T(8,128)S(1)} %get-tuple-element.24), channel_id=1, source_target_pairs={{0,1},{1,0},{2,3},{3,2},{4,5},{5,4},{6,7},{7,6},{8,9},{9,8},{10,11... | collective-permute-start | bytes 430088 | tf_op jit(solution)/shard_map/ppermute | solution.py:35
  45.9 4.0 %collective-permute-start.7 = (f32[24,128]{1,0:T(8,128)S(1)}, f32[24,128]{1,0:T(8,128)S(1)}, u32[]{:S(2)}, u32[]{:S(2)}) collective-permute-start(f32[24,128]{1,0:T(8,128)S(1)} %get-tuple-element.25), channel_id=1, source_target_pairs={{0,1},{1,0},{2,3},{3,2},{4,5},{5,4},{6,7},{7,6},{8,9},{9,8},{10,11... | collective-permute-start | bytes 36872 | tf_op jit(solution)/shard_map/ppermute | solution.py:541
  49.9 1.2 %collective-permute-start.8 = (f32[24,128]{1,0:T(8,128)S(1)}, f32[24,128]{1,0:T(8,128)S(1)}, u32[]{:S(2)}, u32[]{:S(2)}) collective-permute-start(f32[24,128]{1,0:T(8,128)S(1)} %add.12), channel_id=1, source_target_pairs={{0,8},{8,0},{16,24},{24,16},{1,9},{9,1},{17,25},{25,17},{2,10},{10... | collective-permute-start | bytes 36872 | tf_op jit(solution)/shard_map/ppermute | solution.py:541
  51.1 4.7 %collective-permute-start.9 = (f32[24,128]{1,0:T(8,128)S(1)}, f32[24,128]{1,0:T(8,128)S(1)}, u32[]{:S(2)}, u32[]{:S(2)}) collective-permute-start(f32[24,128]{1,0:T(8,128)S(1)} %add.13), channel_id=1, source_target_pairs={{0,16},{8,24},{16,0},{24,8},{1,17},{9,25},{17,1},{25,9},{2,18},{10... | collective-permute-start | bytes 36872 | tf_op jit(solution)/shard_map/ppermute | solution.py:541
  55.8 6.3 %collective-permute-start.10 = (f32[24,128]{1,0:T(8,128)S(1)}, f32[24,128]{1,0:T(8,128)S(1)}, u32[]{:S(2)}, u32[]{:S(2)}) collective-permute-start(f32[24,128]{1,0:T(8,128)S(1)} %add.14), channel_id=1, source_target_pairs={{0,2},{2,0},{4,6},{6,4},{1,3},{3,1},{5,7},{7,5},{8,10},{10,8},{12,... | collective-permute-start | bytes 36872 | tf_op jit(solution)/shard_map/ppermute | solution.py:541
  62.1 5.3 %collective-permute-start.11 = (f32[24,128]{1,0:T(8,128)S(1)}, f32[24,128]{1,0:T(8,128)S(1)}, u32[]{:S(2)}, u32[]{:S(2)}) collective-permute-start(f32[24,128]{1,0:T(8,128)S(1)} %add.15.gram_a), channel_id=1, source_target_pairs={{0,4},{2,6},{4,0},{6,2},{1,5},{3,7},{5,1},{7,3},{8,12},{10,14},{12... | collective-permute-start | bytes 36872 | tf_op jit(solution)/shard_map/ppermute | solution.py:542

commit v3 on v2

--- a/solution.py
+++ b/solution.py
@@ -89,7 +89,7 @@
                 eb_ref[row : row + DEPTH, :] = jnp.where(ey, low, high)
 
 
-def assemble(nx, ny, two_z, pad_in, xa, xb, ya, yb, ea, eb, *outs):
+def assemble(nx, ny, two_z, pad_in, inner, xa, xb, ya, yb, ea, eb, *outs):
     del pad_in
     if two_z:
         pad, own, za, zb = outs
@@ -101,7 +101,7 @@
     bottom = TOP + ny
     wide = nx + 2 * DEPTH
     half = wide // 2
-    tiles = (ny + 2 * DEPTH + 7) // 8
+    tiles = ny // 8 + 1
     for f in range(slabs):
         for i in range(DEPTH):
             a, b = xa[f, i], xb[f, i]
@@ -125,6 +125,7 @@
     is_left = lane % 2 == 1
     column = lane % wide
     step = jnp.minimum(lane // wide, DEPTH - 1)
+    upper = lax.broadcasted_iota(jnp.int32, (8, LANES), 0) < 4
 
     def from_halves(first, second, at, zs):
         in_first = at < half
@@ -134,14 +135,25 @@
     @pl.loop(0, slabs)
     def _(f):
         for t in range(tiles):
-            rows = slice(TOP - DEPTH + 8 * t, TOP - DEPTH + 8 * t + 8)
             packed = []
             for part in range(2):
-                acc = jnp.zeros((8, LANES), F32)
-                for m in range(half):
-                    tile = pad[f, part * half + m, rows, :]
-                    moved = pltpu.roll(tile, 6 * m + 3, 1)
-                    acc = jnp.where(lane // 6 == m, moved, acc)
+                if t < tiles - 1:
+                    acc = inner[f, t, part]
+                    todo = range(DEPTH) if part == 0 else range(half - DEPTH, half)
+                else:
+                    acc = jnp.zeros((8, LANES), F32)
+                    todo = range(half)
+                for m in todo:
+                    plane = part * half + m
+                    if t < tiles - 1:
+                        tile = pad[f, plane, TOP + 8 * t : TOP + 8 * t + 8, :]
+                    else:
+                        tile = jnp.where(
+                            upper,
+                            pad[f, plane, TOP - DEPTH : TOP - DEPTH + 8, :],
+                            pad[f, plane, bottom - 4 : bottom + 4, :],
+                        )
+                    acc = jnp.where(lane // 6 == m, pltpu.roll(tile, 6 * m + 3, 1), acc)
                 packed.append(acc)
             first, second = packed
             out = slice(8 * t, 8 * t + 8)
@@ -157,6 +169,21 @@
                 )
 
 
+def inner_strips(nx, ny, pad, inner):
+    half = nx // 2 + DEPTH
+    lane = lane_index()
+
+    @pl.loop(0, pad.shape[0])
+    def _(f):
+        for t in range(ny // 8):
+            for part in range(2):
+                acc = jnp.zeros((8, LANES), F32)
+                for m in range(DEPTH, half) if part == 0 else range(half - DEPTH):
+                    tile = pad[f, part * half + m, TOP + 8 * t : TOP + 8 * t + 8, :]
+                    acc = jnp.where(lane // 6 == m, pltpu.roll(tile, 6 * m + 3, 1), acc)
+                inner[f, t, part] = acc
+
+
 def face(center, other):
     total = center + other
     return 2.0 * center * other / jnp.where(total > 0, total, 1.0)
@@ -194,7 +221,14 @@
 
     @pl.loop(0, fields + 1)
     def _(f):
-        for t in range(tiles):
+        def put(q, t, tile):
+            if t < ny // 8:
+                strip[f, q, DEPTH + 8 * t : DEPTH + 8 * t + 8, :] = tile
+            else:
+                strip[f, q, 0:DEPTH, :] = tile[0:DEPTH, :]
+                strip[f, q, DEPTH + ny : 2 * DEPTH + ny, :] = tile[4 : 4 + DEPTH, :]
+
+        for t in range(ny // 8 + 1):
             rows = slice(8 * t, 8 * t + 8)
             got_a = za[f, rows, :]
             if two_z:
@@ -208,9 +242,9 @@
                 else:
                     keep = is_left != ez
                     tile = jnp.where(keep, take_lanes(got_a, index), 0.0)
-                strip[f, q, rows, :] = tile
+                put(q, t, tile)
             for j in range(2):
-                strip[f, DEPTH + j, rows, :] = own[f, j, rows, :]
+                put(DEPTH + j, t, own[f, j, rows, :])
 
     def strip_neighbours(ref, f, q, base, row):
         rows = slice(row, row + 8)
@@ -388,10 +422,16 @@
     lane = lax.broadcasted_iota(jnp.int32, (order, LANES), 1)
     work = (gram_a[...] + gram_b[...]) / cells
     work = jnp.where(lane < order, work, jnp.where(lane == row + 64, 1.0, 0.0))
-    for j in range(order):
-        pivot = work[j : j + 1, :]
-        factor = work[:, j : j + 1] / work[j : j + 1, j : j + 1]
-        work = work - jnp.where(row > j, factor * pivot, 0.0)
+    for start in range(0, order, 8):
+        columns = [
+            jnp.broadcast_to(work[:, j : j + 1], (order, LANES)) for j in range(start, start + 8)
+        ]
+        for k in range(8):
+            j = start + k
+            factor = jnp.where(row > j, columns[k] / columns[k][j : j + 1, :], 0.0)
+            work = work - factor * work[j : j + 1, :]
+            for m in range(k + 1, 8):
+                columns[m] = columns[m] - factor * columns[m][j : j + 1, :]
     pivots = jnp.sum(jnp.where(lane == row, work, 0.0), 1, keepdims=True)
     work = work / jnp.sqrt(pivots)
     factor_ref[...] = jnp.where(lane >= row, work, 0.0)[:, :order]
@@ -463,7 +503,7 @@
     rows = 8 * order
     tall = ny + 16
     wide = nx + 2 * DEPTH
-    strip_rows = 8 * ((ny + 2 * DEPTH + 7) // 8)
+    strip_rows = ny + 8
     two_z = lax.axis_size("gz") > 2
     devices = lax.axis_size("gx") * lax.axis_size("gy") * lax.axis_size("gz")
     cells = float(nx * ny * nz * devices)
@@ -479,11 +519,20 @@
         in_specs=[pl.BlockSpec(memory_space=pltpu.HBM)] * 2,
         out_specs=(VM(),) * 5,
         scratch_shapes=[pltpu.SemaphoreType.DMA((slabs,))],
-        compiler_params=params(8),
+        compiler_params=params(46),
         name="pack_faces",
     )(right_sides, permeability)
+    got_ya, got_yb = pair_exchange(ya, yb, "gy")
     got_xa, got_xb = pair_exchange(xa, xb, "gx")
-    got_ya, got_yb = pair_exchange(ya, yb, "gy")
+    inner = pl.pallas_call(
+        functools.partial(inner_strips, nx, ny),
+        out_shape=pltpu.VMEM((slabs, ny // 8, 2, 8, LANES), F32),
+        in_specs=[VM()],
+        out_specs=VM(),
+        compiler_params=params(8),
+        name="inner_strips",
+        cost_estimate=pl.CostEstimate(flops=slabs * nx * ny * nz * 200, bytes_accessed=4 * slabs * nx * ny * nz, transcendentals=0),
+    )(pad)
     ea, eb = pl.pallas_call(
         pack_edges,
         out_shape=(e_type, e_type),
@@ -500,12 +549,12 @@
     outs = pl.pallas_call(
         functools.partial(assemble, nx, ny, two_z),
         out_shape=(pad_type, own_type) + (z_type,) * z_count,
-        in_specs=[VM()] * 7,
+        in_specs=[VM()] * 8,
         out_specs=(VM(),) * (2 + z_count),
         input_output_aliases={0: 0},
         compiler_params=params(8),
         name="assemble",
-    )(pad, got_xa, got_xb, got_ya, got_yb, got_ea, got_eb)
+    )(pad, inner, got_xa, got_xb, got_ya, got_yb, got_ea, got_eb)
     pad, own = outs[:2]
     got_z = pair_exchange(outs[2], outs[-1], "gz")
 

time: 79.1 us -> 74.3 us (0.939)
  local copies, waits for them, and re-layouts: 2.92 us -> 0 us
  waiting for transfers between devices: 13.8 us -> 12.1 us
    unnamed x4 -> x0, local copies, waits for them, and re-layouts: 2.92 us -> none
    pallas_call x1, Pallas kernels: 4.22 us -> 2.21 us  [on_device(): pl.pallas_call(functools.partial(assemble, nx, ny, two_z), out_shape=(pad...]
    ppermute x4, waiting for transfers between devices: 5.87 us -> 4.25 us  [pair_exchange(): lax.ppermute(first, axis, [p for a, b in firsts for p in ((a, b), (b, a))])]
    pallas_call x1, Pallas kernels: 0.54 us -> 2.08 us  [on_device(): pl.pallas_call(pack_faces, out_shape=(pad_type, x_type, x_type, y_type, y...]
    pallas_call x0 -> x1, Pallas kernels: none -> 1.42 us  [on_device(): pl.pallas_call(functools.partial(inner_strips, nx, ny), out_shape=pltpu.V...]
    pallas_call x1, Pallas kernels: 11.5 us -> 10.3 us  [on_device(): pl.pallas_call(functools.partial(factor_and_solve, cells, order, nx, ny),...]
  transfers between devices with their start and end apart: 12 -> 12, of which waited for: 8 -> 7; matrix products, arithmetic and copies ran while one was open for 0% -> 0% of each run, Pallas kernels for 0% -> 2%
where the time goes in v3:
time: 74.3 us; the launch traced here: 74.2 us
  Pallas kernels  35.7 us (48%)
  starting transfers between devices  25.6 us (34%)
  waiting for transfers between devices  12.1 us (16%)
    pallas_call x1, Pallas kernels, on_device(): pl.pallas_call(functools.partial(powers, nx, ny, two_z), out_shape=(split...  19.7 us
    pallas_call x1, Pallas kernels, on_device(): pl.pallas_call(functools.partial(factor_and_solve, cells, order, nx, ny),...  10.3 us
    ppermute x4, starting transfers between devices, on_device(): gram = gram + lax.ppermute(gram, axis, pairs)  10.1 us
    ppermute x4, starting transfers between devices, pair_exchange(): lax.ppermute(first, axis, [p for a, b in firsts for p in ((a, b), (b, a))])  9.94 us
    ppermute x4, waiting for transfers between devices, on_device(): gram = gram + lax.ppermute(gram, axis, pairs)  6.2 us
    ppermute x4, waiting for transfers between devices, pair_exchange(): lax.ppermute(first, axis, [p for a, b in firsts for p in ((a, b), (b, a))])  4.25 us
    ppermute x1, starting transfers between devices, on_device(): other = lax.ppermute(gram, *stages[-1])  3.58 us
    pallas_call x1, Pallas kernels, on_device(): pl.pallas_call(functools.partial(assemble, nx, ny, two_z), out_shape=(pad...  2.21 us
  transfers between devices with their start and end apart: 12, of which 7 were waited for; matrix products, arithmetic and copies ran while one was open for 0% of the time, Pallas kernels for 2%

profile of v3, /device:TPU:0, one launch (start us, length us, event | category | flops | bytes accessed | tf_op | source)
XLA Modules:
  0.0 74.2 jit_solution(16723019230942532789)
XLA Ops:
  0.6 2.1 %pack_faces.1 = (f32[7,38,48,128]{3,2,1,0:T(8,128)S(1)}, f32[7,3,32,128]{3,2,1,0:T(8,128)S(1)}, f32[7,3,32,128]{3,2,1,0:T(8,128)S(1)}, f32[672,128]{1,0:T(8,128)S(1)}, f32[672,128]{1,0:T(8,128)S(1)}) custom-call(f32[6,32,32,128]{3,2,1,0:T(8,128)} %rs_ref.1, f32[32,32,128]{2,1,0:T(8,128)} %k_ref.1), custom_call_target="tpu_custom_call" | custom-call | tf_op jit(solution)/shard_map/pack_faces/pallas_call | solution.py:516
  2.7 0.6 collective-permute-start
  3.3 0.7 collective-permute-start.1
  4.0 2.6 %collective-permute-start.2 = (f32[672,128]{1,0:T(8,128)S(1)}, f32[672,128]{1,0:T(8,128)S(1)}, u32[]{:S(2)}, u32[]{:S(2)}) collective-permute-start(f32[672,128]{1,0:T(8,128)S(1)} %get-tuple-element.18), channel_id=1, source_target_pairs={{0,2},{2,0},{4,6},{6,4},{1,3},{3,1},{5,7},{7,5},{8,10},{10,8},{12,... | collective-permute-start | bytes 1032200 | tf_op jit(solution)/shard_map/ppermute | solution.py:35
  6.6 0.7 collective-permute-start.3
  7.3 0.0 collective-permute-done.xa_ref.xa
  7.4 4.4 %collective-permute-start.4 = (f32[128,128]{1,0:T(8,128)S(1)}, f32[128,128]{1,0:T(8,128)S(1)}, u32[]{:S(2)}, u32[]{:S(2)}) collective-permute-start(f32[128,128]{1,0:T(8,128)S(1)} %get-tuple-element.20), channel_id=1, source_target_pairs={{0,2},{2,0},{4,6},{6,4},{1,3},{3,1},{5,7},{7,5},{8,10},{10,8},{12,... | collective-permute-start | bytes 196616 | tf_op jit(solution)/shard_map/ppermute | solution.py:35
  11.8 0.7 collective-permute-start.5
  12.5 1.4 %inner_strips.1.inner = f32[7,4,2,8,128]{4,3,2,1,0:T(8,128)S(1)} custom-call(f32[7,38,48,128]{3,2,1,0:T(8,128)S(1)} %get-tuple-element.15.pad.pad_in), custom_call_target="tpu_custom_call" | custom-call | flops 183500800 | bytes 3670016 | tf_op jit(solution)/shard_map/inner_strips/pallas_call | solution.py:527
  13.9 0.8 %collective-permute-done.4.ea = f32[128,128]{1,0:T(8,128)S(1)} collective-permute-done((f32[128,128]{1,0:T(8,128)S(1)}, f32[128,128]{1,0:T(8,128)S(1)}, u32[]{:S(2)}, u32[]{:S(2)}) %collective-permute-start.4) | collective-permute-done | bytes 65568 | tf_op jit(solution)/shard_map/ppermute | solution.py:35
  14.8 2.2 %assemble.1 = (f32[7,38,48,128]{3,2,1,0:T(8,128)S(1)}, f32[7,2,40,128]{3,2,1,0:T(8,128)S(1)}, f32[7,40,128]{2,1,0:T(8,128)S(1)}) custom-call(f32[7,38,48,128]{3,2,1,0:T(8,128)S(1)} %get-tuple-element.15.pad.pad_in, f32[7,4,2,8,128]{4,3,2,1,0:T(8,128)S(1)} %inner_strips.1.inner, ...), custom_call_target="tpu_custom_call", output_to_operand_aliasing={{0}: (0, {})} | custom-call | tf_op jit(solution)/shard_map/assemble/pallas_call | solution.py:549
  17.0 2.3 %collective-permute-start.6 = (f32[7,40,128]{2,1,0:T(8,128)S(1)}, f32[7,40,128]{2,1,0:T(8,128)S(1)}, u32[]{:S(2)}, u32[]{:S(2)}) collective-permute-start(f32[7,40,128]{2,1,0:T(8,128)S(1)} %get-tuple-element.24), channel_id=1, source_target_pairs={{0,1},{1,0},{2,3},{3,2},{4,5},{5,4},{6,7},{7,6},{8,9},{9,8},{10,11... | collective-permute-start | bytes 430088 | tf_op jit(solution)/shard_map/ppermute | solution.py:35
  19.3 3.4 %collective-permute-done.6.za = f32[7,40,128]{2,1,0:T(8,128)S(1)} collective-permute-done((f32[7,40,128]{2,1,0:T(8,128)S(1)}, f32[7,40,128]{2,1,0:T(8,128)S(1)}, u32[]{:S(2)}, u32[]{:S(2)}) %collective-permute-start.6) | collective-permute-done | bytes 143392 | tf_op jit(solution)/shard_map/ppermute | solution.py:35
  22.7 19.7 %powers.1 = (bf16[128,192,128]{2,1,0:T(8,128)(2,1)S(1)}, bf16[128,192,128]{2,1,0:T(8,128)(2,1)S(1)}, f32[24,128]{1,0:T(8,128)S(1)}) custom-call(f32[7,38,48,128]{3,2,1,0:T(8,128)S(1)} %get-tuple-element.22.pad, f32[7,2,40,128]{3,2,1,0:T(8,128)S(1)} %get-tuple-element.23.own, f32[7,40,128]{2,1,0:T(8,128)S(1)} %collective-permute-done.6.za), custom_call_target="tpu_custom_call" | custom-call | tf_op jit(solution)/shard_map/powers/pallas_call | solution.py:563
  42.4 2.5 %collective-permute-start.7 = (f32[24,128]{1,0:T(8,128)S(1)}, f32[24,128]{1,0:T(8,128)S(1)}, u32[]{:S(2)}, u32[]{:S(2)}) collective-permute-start(f32[24,128]{1,0:T(8,128)S(1)} %get-tuple-element.25), channel_id=1, source_target_pairs={{0,1},{1,0},{2,3},{3,2},{4,5},{5,4},{6,7},{7,6},{8,9},{9,8},{10,11... | collective-permute-start | bytes 36872 | tf_op jit(solution)/shard_map/ppermute | solution.py:590
  44.9 1.7 %collective-permute-done.7 = f32[24,128]{1,0:T(8,128)S(1)} collective-permute-done((f32[24,128]{1,0:T(8,128)S(1)}, f32[24,128]{1,0:T(8,128)S(1)}, u32[]{:S(2)}, u32[]{:S(2)}) %collective-permute-start.7) | collective-permute-done | bytes 12320 | tf_op jit(solution)/shard_map/ppermute | solution.py:590
  46.5 1.2 %collective-permute-done.8 = f32[24,128]{1,0:T(8,128)S(1)} collective-permute-done((f32[24,128]{1,0:T(8,128)S(1)}, f32[24,128]{1,0:T(8,128)S(1)}, u32[]{:S(2)}, u32[]{:S(2)}) %collective-permute-start.8) | collective-permute-done | bytes 12320 | tf_op jit(solution)/shard_map/ppermute | solution.py:590
  47.7 3.0 %collective-permute-start.9 = (f32[24,128]{1,0:T(8,128)S(1)}, f32[24,128]{1,0:T(8,128)S(1)}, u32[]{:S(2)}, u32[]{:S(2)}) collective-permute-start(f32[24,128]{1,0:T(8,128)S(1)} %add.13), channel_id=1, source_target_pairs={{0,16},{8,24},{16,0},{24,8},{1,17},{9,25},{17,1},{25,9},{2,18},{10... | collective-permute-start | bytes 36872 | tf_op jit(solution)/shard_map/ppermute | solution.py:590
  50.7 1.7 %collective-permute-done.9 = f32[24,128]{1,0:T(8,128)S(1)} collective-permute-done((f32[24,128]{1,0:T(8,128)S(1)}, f32[24,128]{1,0:T(8,128)S(1)}, u32[]{:S(2)}, u32[]{:S(2)}) %collective-permute-start.9) | collective-permute-done | bytes 12320 | tf_op jit(solution)/shard_map/ppermute | solution.py:590
  52.4 4.6 %collective-permute-start.10 = (f32[24,128]{1,0:T(8,128)S(1)}, f32[24,128]{1,0:T(8,128)S(1)}, u32[]{:S(2)}, u32[]{:S(2)}) collective-permute-start(f32[24,128]{1,0:T(8,128)S(1)} %add.14), channel_id=1, source_target_pairs={{0,2},{2,0},{4,6},{6,4},{1,3},{3,1},{5,7},{7,5},{8,10},{10,8},{12,... | collective-permute-start | bytes 36872 | tf_op jit(solution)/shard_map/ppermute | solution.py:590
  57.0 1.7 %collective-permute-done.10 = f32[24,128]{1,0:T(8,128)S(1)} collective-permute-done((f32[24,128]{1,0:T(8,128)S(1)}, f32[24,128]{1,0:T(8,128)S(1)}, u32[]{:S(2)}, u32[]{:S(2)}) %collective-permute-start.10) | collective-permute-done | bytes 12320 | tf_op jit(solution)/shard_map/ppermute | solution.py:590
  58.7 3.6 %collective-permute-start.11 = (f32[24,128]{1,0:T(8,128)S(1)}, f32[24,128]{1,0:T(8,128)S(1)}, u32[]{:S(2)}, u32[]{:S(2)}) collective-permute-start(f32[24,128]{1,0:T(8,128)S(1)} %add.15.gram_a), channel_id=1, source_target_pairs={{0,4},{2,6},{4,0},{6,2},{1,5},{3,7},{5,1},{7,3},{8,12},{10,14},{12... | collective-permute-start | bytes 36872 | tf_op jit(solution)/shard_map/ppermute | solution.py:591
  62.3 1.7 %collective-permute-done.11.gram_b = f32[24,128]{1,0:T(8,128)S(1)} collective-permute-done((f32[24,128]{1,0:T(8,128)S(1)}, f32[24,128]{1,0:T(8,128)S(1)}, u32[]{:S(2)}, u32[]{:S(2)}) %collective-permute-start.11) | collective-permute-done | bytes 12320 | tf_op jit(solution)/shard_map/ppermute | solution.py:591
  63.9 10.3 %factor_and_solve.1 = (f32[24,32,32,128]{3,2,1,0:T(8,128)}, f32[24,24]{1,0:T(8,128)}) custom-call(f32[24,128]{1,0:T(8,128)S(1)} %add.15.gram_a, f32[24,128]{1,0:T(8,128)S(1)} %collective-permute-done.11.gram_b, bf16[128,192,128]{2,1,0:T(8,128)(2,1)S(1)} %get-tuple-element.26.high_ref, bf16[128,192,128]{2,1,0:T(8,128)(2,1)S(1)} %get-tuple-element.27.low_ref), custom_call_target="tpu_custom_call" | custom-call | tf_op jit(solution)/shard_map/factor_and_solve/pallas_call | solution.py:593
  (10 shorter events, 0.1 us)
Async XLA Ops:
  2.7 4.6 %collective-permute-start = (f32[7,3,32,128]{3,2,1,0:T(8,128)S(1)}, f32[7,3,32,128]{3,2,1,0:T(8,128)S(1)}, u32[]{:S(2)}, u32[]{:S(2)}) collective-permute-start(f32[7,3,32,128]{3,2,1,0:T(8,128)S(1)} %get-tuple-element.16), channel_id=1, source_target_pairs={{0,8},{8,0},{16,24},{24,16},{1,9},{9,1},{17,25},{25,17},{2,10},{10... | collective-permute-start | bytes 1032200 | tf_op jit(solution)/shard_map/ppermute | solution.py:35
  3.3 4.0 %collective-permute-start.1 = (f32[7,3,32,128]{3,2,1,0:T(8,128)S(1)}, f32[7,3,32,128]{3,2,1,0:T(8,128)S(1)}, u32[]{:S(2)}, u32[]{:S(2)}) collective-permute-start(f32[7,3,32,128]{3,2,1,0:T(8,128)S(1)} %get-tuple-element.17), channel_id=1, source_target_pairs={{8,16},{16,8},{9,17},{17,9},{10,18},{18,10},{11,19},{19,11},{12,20... | collective-permute-start | bytes 1032200 | tf_op jit(solution)/shard_map/ppermute | solution.py:38
  4.0 9.9 %collective-permute-start.2 = (f32[672,128]{1,0:T(8,128)S(1)}, f32[672,128]{1,0:T(8,128)S(1)}, u32[]{:S(2)}, u32[]{:S(2)}) collective-permute-start(f32[672,128]{1,0:T(8,128)S(1)} %get-tuple-element.18), channel_id=1, source_target_pairs={{0,2},{2,0},{4,6},{6,4},{1,3},{3,1},{5,7},{7,5},{8,10},{10,8},{12,... | collective-permute-start | bytes 1032200 | tf_op jit(solution)/shard_map/ppermute | solution.py:35
  6.6 7.3 %collective-permute-start.3 = (f32[672,128]{1,0:T(8,128)S(1)}, f32[672,128]{1,0:T(8,128)S(1)}, u32[]{:S(2)}, u32[]{:S(2)}) collective-permute-start(f32[672,128]{1,0:T(8,128)S(1)} %get-tuple-element.19), channel_id=1, source_target_pairs={{2,4},{4,2},{3,5},{5,3},{10,12},{12,10},{11,13},{13,11},{18,20},{2... | collective-permute-start | bytes 1032200 | tf_op jit(solution)/shard_map/ppermute | solution.py:38
  7.4 7.4 %collective-permute-start.4 = (f32[128,128]{1,0:T(8,128)S(1)}, f32[128,128]{1,0:T(8,128)S(1)}, u32[]{:S(2)}, u32[]{:S(2)}) collective-permute-start(f32[128,128]{1,0:T(8,128)S(1)} %get-tuple-element.20), channel_id=1, source_target_pairs={{0,2},{2,0},{4,6},{6,4},{1,3},{3,1},{5,7},{7,5},{8,10},{10,8},{12,... | collective-permute-start | bytes 196616 | tf_op jit(solution)/shard_map/ppermute | solution.py:35
  11.8 2.9 %collective-permute-start.5 = (f32[128,128]{1,0:T(8,128)S(1)}, f32[128,128]{1,0:T(8,128)S(1)}, u32[]{:S(2)}, u32[]{:S(2)}) collective-permute-start(f32[128,128]{1,0:T(8,128)S(1)} %get-tuple-element.21), channel_id=1, source_target_pairs={{2,4},{4,2},{3,5},{5,3},{10,12},{12,10},{11,13},{13,11},{18,20},{2... | collective-permute-start | bytes 196616 | tf_op jit(solution)/shard_map/ppermute | solution.py:38
  17.0 5.7 %collective-permute-start.6 = (f32[7,40,128]{2,1,0:T(8,128)S(1)}, f32[7,40,128]{2,1,0:T(8,128)S(1)}, u32[]{:S(2)}, u32[]{:S(2)}) collective-permute-start(f32[7,40,128]{2,1,0:T(8,128)S(1)} %get-tuple-element.24), channel_id=1, source_target_pairs={{0,1},{1,0},{2,3},{3,2},{4,5},{5,4},{6,7},{7,6},{8,9},{9,8},{10,11... | collective-permute-start | bytes 430088 | tf_op jit(solution)/shard_map/ppermute | solution.py:35
  42.4 4.2 %collective-permute-start.7 = (f32[24,128]{1,0:T(8,128)S(1)}, f32[24,128]{1,0:T(8,128)S(1)}, u32[]{:S(2)}, u32[]{:S(2)}) collective-permute-start(f32[24,128]{1,0:T(8,128)S(1)} %get-tuple-element.25), channel_id=1, source_target_pairs={{0,1},{1,0},{2,3},{3,2},{4,5},{5,4},{6,7},{7,6},{8,9},{9,8},{10,11... | collective-permute-start | bytes 36872 | tf_op jit(solution)/shard_map/ppermute | solution.py:590
  46.5 1.2 %collective-permute-start.8 = (f32[24,128]{1,0:T(8,128)S(1)}, f32[24,128]{1,0:T(8,128)S(1)}, u32[]{:S(2)}, u32[]{:S(2)}) collective-permute-start(f32[24,128]{1,0:T(8,128)S(1)} %add.12), channel_id=1, source_target_pairs={{0,8},{8,0},{16,24},{24,16},{1,9},{9,1},{17,25},{25,17},{2,10},{10... | collective-permute-start | bytes 36872 | tf_op jit(solution)/shard_map/ppermute | solution.py:590
  47.7 4.7 %collective-permute-start.9 = (f32[24,128]{1,0:T(8,128)S(1)}, f32[24,128]{1,0:T(8,128)S(1)}, u32[]{:S(2)}, u32[]{:S(2)}) collective-permute-start(f32[24,128]{1,0:T(8,128)S(1)} %add.13), channel_id=1, source_target_pairs={{0,16},{8,24},{16,0},{24,8},{1,17},{9,25},{17,1},{25,9},{2,18},{10... | collective-permute-start | bytes 36872 | tf_op jit(solution)/shard_map/ppermute | solution.py:590
  52.4 6.3 %collective-permute-start.10 = (f32[24,128]{1,0:T(8,128)S(1)}, f32[24,128]{1,0:T(8,128)S(1)}, u32[]{:S(2)}, u32[]{:S(2)}) collective-permute-start(f32[24,128]{1,0:T(8,128)S(1)} %add.14), channel_id=1, source_target_pairs={{0,2},{2,0},{4,6},{6,4},{1,3},{3,1},{5,7},{7,5},{8,10},{10,8},{12,... | collective-permute-start | bytes 36872 | tf_op jit(solution)/shard_map/ppermute | solution.py:590
  58.7 5.3 %collective-permute-start.11 = (f32[24,128]{1,0:T(8,128)S(1)}, f32[24,128]{1,0:T(8,128)S(1)}, u32[]{:S(2)}, u32[]{:S(2)}) collective-permute-start(f32[24,128]{1,0:T(8,128)S(1)} %add.15.gram_a), channel_id=1, source_target_pairs={{0,4},{2,6},{4,0},{6,2},{1,5},{3,7},{5,1},{7,3},{8,12},{10,14},{12... | collective-permute-start | bytes 36872 | tf_op jit(solution)/shard_map/ppermute | solution.py:591

commit v4 on v3

--- a/solution.py
+++ b/solution.py
@@ -13,7 +13,7 @@
 LANES = 128
 TOP = 8
 MIB = 1 << 20
-TOGETHER = 2
+TOGETHER = 4
 
 
 def even_on(axis):
@@ -189,6 +189,30 @@
     return 2.0 * center * other / jnp.where(total > 0, total, 1.0)
 
 
+def plane_faces(nx, ny, pad, faces):
+    fields = pad.shape[0] - 1
+    lane = lane_index()
+
+    @pl.loop(0, nx + 4, unroll=2)
+    def _(i):
+        plane = i + 1
+        for t in range((ny + 2 * DEPTH + 7) // 8):
+            r = TOP - 2 + 8 * t
+            tile = pad[fields, plane, r : r + 8, :]
+            beside = face(tile, pltpu.roll(tile, LANES - 1, 1))
+            beside = jnp.where(lane == LANES - 1, 0.0, beside)
+            found = [
+                face(tile, pad[fields, plane + 1, r : r + 8, :]),
+                face(tile, pad[fields, plane - 1, r : r + 8, :]),
+                face(tile, pad[fields, plane, r + 1 : r + 9, :]),
+                face(tile, pad[fields, plane, r - 1 : r + 7, :]),
+                beside,
+                pltpu.roll(beside, 1, 1),
+            ]
+            for n, weight in enumerate(found):
+                faces[n, i, 8 * t : 8 * t + 8, :] = weight
+
+
 def scaled_faces(center, others):
     faces = [face(center, other) for other in others]
     diagonal = faces[0]
@@ -205,12 +229,12 @@
     return accum
 
 
-def powers(nx, ny, two_z, pad, own, za, *rest):
+def powers(nx, ny, two_z, pad, own, faces, za, *rest):
     if two_z:
         zb, rest = rest[0], rest[1:]
     else:
         zb = None
-    high_ref, low_ref, gram_ref, coef, v1, v2, strip, scoef, s1, s2, acc, square = rest
+    high_ref, low_ref, gram_ref, coef, v1, v2, strip, scoef, s1, s2, acc, square, edge = rest
     fields = pad.shape[0] - 1
     wide = nx + 2 * DEPTH
     ez = even_on("gz")
@@ -279,30 +303,60 @@
             _, values = strip_neighbours(s1, f, 2, 1, row)
             s2[f, row : row + 8, :] = weighted(weights, values)
 
-    def z_pair(tile, edge, plane):
-        moved = pltpu.roll(edge, LANES - 1 - 2 * plane, 1)
-        return [
-            jnp.where(lane == LANES - 1, moved, pltpu.roll(tile, LANES - 1, 1)),
-            jnp.where(lane == 0, moved, pltpu.roll(tile, 1, 1)),
-        ]
-
-    @pl.loop(0, nx + 4)
+    def fill(base, count, y, lag, values_at):
+        for t in range(count):
+            row = y + DEPTH + 8 * t
+            weight = scoef[5, 2, row : row + 8, :]
+            for g in range(fields // 2):
+                pair = [
+                    pltpu.roll(weight * values_at(f, slice(row, row + 8)), 2 * lag, 1)
+                    if lag
+                    else weight * values_at(f, slice(row, row + 8))
+                    for f in (2 * g, 2 * g + 1)
+                ]
+                pair = jnp.concatenate(pair, 0)
+                high = pair.astype(BF16)
+                at = base + 8 * (t * fields + 2 * g)
+                edge[at : at + 16, :LANES] = high
+                edge[at : at + 16, LANES:] = (pair - high.astype(F32)).astype(BF16)
+
+    base2 = fields * ny
+    base1 = base2 + 8 * fields * tiles
+    ends = base1 + 8 * fields * tiles
+    fill(0, ny // 8, 0, 4, lambda f, rows: s2[f, rows, :])
+    fill(base2, tiles, -1, 2, lambda f, rows: s1[f, 1, rows, :])
+    fill(base1, tiles, -2, 0, lambda f, rows: strip[f, 2, rows, :])
+
+    def chosen(front):
+        lanes = lane_index(LANES)
+        source = jnp.where(
+            lanes == 0, 2 * front + 1, jnp.where(lanes == LANES - 1, 2 * front, -1)
+        )
+        one_hot = lax.broadcasted_iota(jnp.int32, (LANES, LANES), 0) == source
+        one_hot = jnp.where(one_hot, 1.0, 0.0).astype(BF16)
+        return jnp.concatenate([one_hot, one_hot], 0)
+
+    def beyond(front, start, stop):
+        return jnp.dot(edge[start:stop, :], chosen(front), preferred_element_type=F32)
+
+    @pl.loop(0, nx + 4, unroll=4)
     def _(i):
         plane = i + 1
         for t in range(tiles):
             y = 8 * t - 2
-            r = TOP + y
-            tile = pad[fields, plane, r : r + 8, :]
-            others = [
-                pad[fields, plane + 1, r : r + 8, :],
-                pad[fields, plane - 1, r : r + 8, :],
-                pad[fields, plane, r + 1 : r + 9, :],
-                pad[fields, plane, r - 1 : r + 7, :],
-            ] + z_pair(tile, strip[fields, 2, y + 3 : y + 11, :], plane)
-            for n, weight in enumerate(scaled_faces(tile, others)):
-                coef[n, i, 8 * t : 8 * t + 8, :] = weight
-
-    def advance(source, source_x, edge, f, plane, y, weights):
+            tile = pad[fields, plane, TOP + y : TOP + y + 8, :]
+            outside = pltpu.roll(strip[fields, 2, y + 3 : y + 11, :], LANES - 1 - 2 * plane, 1)
+            weights = [faces[n, i, 8 * t : 8 * t + 8, :] for n in range(6)]
+            diagonal = jnp.where(
+                (lane == 0) | (lane == LANES - 1), face(tile, outside), 0.0
+            )
+            for weight in weights:
+                diagonal = diagonal + weight
+            scale = 2.5 / jnp.where(diagonal > 0, diagonal, 1.0)
+            for n, weight in enumerate(weights):
+                coef[n, i, 8 * t : 8 * t + 8, :] = weight * scale
+
+    def advance(source, source_x, extra, f, plane, y, weights):
         r = TOP + y
         s = plane - source_x
         tile = source[f, s, r : r + 8, :]
@@ -311,35 +365,39 @@
             source[f, s - 1, r : r + 8, :],
             source[f, s, r + 1 : r + 9, :],
             source[f, s, r - 1 : r + 7, :],
-        ] + z_pair(tile, edge, plane)
-        return weighted(weights, values)
+            pltpu.roll(tile, LANES - 1, 1),
+            pltpu.roll(tile, 1, 1),
+        ]
+        return weighted(weights, values) + extra
 
     def weights_at(plane, y):
         return [coef[n, plane - 1, y + 2 : y + 10, :] for n in range(6)]
 
-    def first_power(plane):
+    def extra_of(terms, t, f):
+        at = 8 * (t * fields + f)
+        return terms[at : at + 8, :]
+
+    def first_power(plane, terms):
         for t in range(tiles):
             y = 8 * t - 2
             weights = weights_at(plane, y)
             for f in range(fields):
-                edge = strip[f, 2, y + 3 : y + 11, :]
                 v1[f, plane - 1, TOP + y : TOP + y + 8, :] = advance(
-                    pad, 0, edge, f, plane, y, weights
+                    pad, 0, extra_of(terms, t, f), f, plane, y, weights
                 )
 
-    def second_power(plane):
+    def second_power(plane, terms):
         for t in range(tiles):
             y = 8 * t - 1
             weights = weights_at(plane, y)
             for f in range(fields):
-                edge = s1[f, 1, y + 3 : y + 11, :]
                 v2[f, plane - 2, TOP + y : TOP + y + 8, :] = advance(
-                    v1, 1, edge, f, plane, y, weights
+                    v1, 1, extra_of(terms, t, f), f, plane, y, weights
                 )
 
     blocks = ny // 8
 
-    def last_power(plane):
+    def last_power(plane, terms):
         for t in range(blocks):
             y = 8 * t
             rows = slice(TOP + y, TOP + y + 8)
@@ -348,8 +406,7 @@
             columns += [v1[f, plane - 1, rows, :] for f in range(fields)]
             columns += [v2[f, plane - 2, rows, :] for f in range(fields)]
             for f in range(fields):
-                edge = s2[f, y + 3 : y + 11, :]
-                columns.append(advance(v2, 2, edge, f, plane, y, weights))
+                columns.append(advance(v2, 2, extra_of(terms, t, f), f, plane, y, weights))
             block = (plane - DEPTH) * blocks + t
             for g in range(len(columns) // 2):
                 pair = jnp.concatenate(columns[2 * g : 2 * g + 2], 0)
@@ -369,30 +426,40 @@
     acc[...] = jnp.zeros_like(acc)
 
     @pl.loop(1, 4)
-    def _(plane):
-        first_power(plane)
+    def _(front):
+        first_power(front, beyond(front, base1, ends))
 
     @pl.loop(4, 7)
-    def _(plane):
-        second_power(plane - 2)
-        first_power(plane)
-
-    last_power(3)
-    second_power(5)
-    first_power(7)
-
-    @pl.loop(8, nx + 5)
-    def _(plane):
-        products(plane - 5)
-        last_power(plane - 4)
-        second_power(plane - 2)
-        first_power(plane)
-
+    def _(front):
+        terms = beyond(front, base2, ends)
+        second_power(front - 2, terms[: base1 - base2])
+        first_power(front, terms[base1 - base2 :])
+
+    def whole_wave(front):
+        terms = beyond(front, 0, ends)
+        last_power(front - 4, terms[:base2])
+        second_power(front - 2, terms[base2:base1])
+        first_power(front, terms[base1:])
+
+    whole_wave(7)
+
+    whole_wave(8)
+    products(3)
+
+    @pl.loop(0, (nx - 4) // 2)
+    def _(step):
+        front = 9 + 2 * step
+        whole_wave(front)
+        products(front - 5)
+        whole_wave(front + 1)
+        products(front - 4)
+
+    terms = beyond(nx + 5, 0, base1)
+    last_power(nx + 1, terms[:base2])
+    second_power(nx + 3, terms[base2:])
     products(nx)
-    last_power(nx + 1)
-    second_power(nx + 3)
+    last_power(nx + 2, beyond(nx + 6, 0, base2))
     products(nx + 1)
-    last_power(nx + 2)
     products(nx + 2)
 
     rows = acc.shape[1]
@@ -558,12 +625,24 @@
     pad, own = outs[:2]
     got_z = pair_exchange(outs[2], outs[-1], "gz")
 
+    faces = pl.pallas_call(
+        functools.partial(plane_faces, nx, ny),
+        out_shape=pltpu.VMEM((6, nx + 4, tall, LANES), F32),
+        in_specs=[VM()],
+        out_specs=VM(),
+        compiler_params=params(8),
+        name="plane_faces",
+        cost_estimate=pl.CostEstimate(
+            flops=nx * ny * nz * 2000, bytes_accessed=28 * nx * ny * nz, transcendentals=0
+        ),
+    )(pad)
+
     blocks = nx * ny // 8
     split_type = pltpu.VMEM((blocks, rows, LANES), BF16)
     high, low, gram = pl.pallas_call(
         functools.partial(powers, nx, ny, two_z),
         out_shape=(split_type, split_type, pltpu.VMEM((order, LANES), F32)),
-        in_specs=[VM()] * (2 + len(got_z)),
+        in_specs=[VM()] * (3 + len(got_z)),
         out_specs=(VM(),) * 3,
         scratch_shapes=[
             pltpu.VMEM((6, nx + 4, tall, LANES), F32),
@@ -575,10 +654,11 @@
             pltpu.VMEM((fields, tall, LANES), F32),
             pltpu.VMEM((2 * rows, rows), F32),
             pltpu.VMEM((LANES, LANES), F32),
+            pltpu.VMEM((fields * (ny + 2 * strip_rows), 2 * LANES), BF16),
         ],
         compiler_params=params(26),
         name="powers",
-    )(pad, own, *got_z)
+    )(pad, own, faces, *got_z)
 
     stages = []
     for axis in ("gz", "gx", "gy"):

time: 74.3 us -> 69.2 us (0.931)
  waiting for transfers between devices: 12.1 us -> 9.31 us
  Pallas kernels: 35.7 us -> 33.3 us
    pallas_call x1, Pallas kernels: 19.7 us -> 15.6 us  [on_device(): pl.pallas_call(functools.partial(powers, nx, ny, two_z), out_shape=(split...]
    ppermute x4, waiting for transfers between devices: 4.25 us -> 1.43 us  [pair_exchange(): lax.ppermute(first, axis, [p for a, b in firsts for p in ((a, b), (b, a))])]
    pallas_call x0 -> x1, Pallas kernels: none -> 2.82 us  [on_device(): pl.pallas_call(functools.partial(plane_faces, nx, ny), out_shape=pltpu.VM...]
    pallas_call x1, Pallas kernels: 10.3 us -> 9.17 us  [on_device(): pl.pallas_call(functools.partial(factor_and_solve, cells, order, nx, ny),...]
  transfers between devices with their start and end apart: 12 -> 12, of which waited for: 7 -> 7; matrix products, arithmetic and copies ran while one was open for 0% -> 0% of each run, Pallas kernels for 2% -> 6%
where the time goes in v4:
time: 69.2 us; the launch traced here: 69 us
  Pallas kernels  33.3 us (48%)
  starting transfers between devices  25.6 us (37%)
  waiting for transfers between devices  9.31 us (13%)
  between operations  0.73 us (1%)
    pallas_call x1, Pallas kernels, on_device(): pl.pallas_call(functools.partial(powers, nx, ny, two_z), out_shape=(split...  15.6 us
    ppermute x4, starting transfers between devices, on_device(): gram = gram + lax.ppermute(gram, axis, pairs)  10.1 us
    ppermute x4, starting transfers between devices, pair_exchange(): lax.ppermute(first, axis, [p for a, b in firsts for p in ((a, b), (b, a))])  9.94 us
    pallas_call x1, Pallas kernels, on_device(): pl.pallas_call(functools.partial(factor_and_solve, cells, order, nx, ny),...  9.17 us
    ppermute x4, waiting for transfers between devices, on_device(): gram = gram + lax.ppermute(gram, axis, pairs)  6.2 us
    ppermute x1, starting transfers between devices, on_device(): other = lax.ppermute(gram, *stages[-1])  3.58 us
    pallas_call x1, Pallas kernels, on_device(): pl.pallas_call(functools.partial(plane_faces, nx, ny), out_shape=pltpu.VM...  2.82 us
    pallas_call x1, Pallas kernels, on_device(): pl.pallas_call(functools.partial(assemble, nx, ny, two_z), out_shape=(pad...  2.21 us
  transfers between devices with their start and end apart: 12, of which 7 were waited for; matrix products, arithmetic and copies ran while one was open for 0% of the time, Pallas kernels for 6%

profile of v4, /device:TPU:0, one launch (start us, length us, event | category | flops | bytes accessed | tf_op | source)
XLA Modules:
  0.0 69.0 jit_solution(3173637932141909335)
XLA Ops:
  0.6 2.1 %pack_faces.1 = (f32[7,38,48,128]{3,2,1,0:T(8,128)S(1)}, f32[7,3,32,128]{3,2,1,0:T(8,128)S(1)}, f32[7,3,32,128]{3,2,1,0:T(8,128)S(1)}, f32[672,128]{1,0:T(8,128)S(1)}, f32[672,128]{1,0:T(8,128)S(1)}) custom-call(f32[6,32,32,128]{3,2,1,0:T(8,128)} %rs_ref.1, f32[32,32,128]{2,1,0:T(8,128)} %k_ref.1), custom_call_target="tpu_custom_call" | custom-call | tf_op jit(solution)/shard_map/pack_faces/pallas_call | solution.py:583
  2.7 0.6 collective-permute-start
  3.3 0.7 collective-permute-start.1
  4.0 2.6 %collective-permute-start.2 = (f32[672,128]{1,0:T(8,128)S(1)}, f32[672,128]{1,0:T(8,128)S(1)}, u32[]{:S(2)}, u32[]{:S(2)}) collective-permute-start(f32[672,128]{1,0:T(8,128)S(1)} %get-tuple-element.18), channel_id=1, source_target_pairs={{0,2},{2,0},{4,6},{6,4},{1,3},{3,1},{5,7},{7,5},{8,10},{10,8},{12,... | collective-permute-start | bytes 1032200 | tf_op jit(solution)/shard_map/ppermute | solution.py:35
  6.6 0.7 collective-permute-start.3
  7.4 4.4 %collective-permute-start.4 = (f32[128,128]{1,0:T(8,128)S(1)}, f32[128,128]{1,0:T(8,128)S(1)}, u32[]{:S(2)}, u32[]{:S(2)}) collective-permute-start(f32[128,128]{1,0:T(8,128)S(1)} %get-tuple-element.20), channel_id=1, source_target_pairs={{0,2},{2,0},{4,6},{6,4},{1,3},{3,1},{5,7},{7,5},{8,10},{10,8},{12,... | collective-permute-start | bytes 196616 | tf_op jit(solution)/shard_map/ppermute | solution.py:35
  11.8 0.7 collective-permute-start.5
  12.5 1.4 %inner_strips.1.inner = f32[7,4,2,8,128]{4,3,2,1,0:T(8,128)S(1)} custom-call(f32[7,38,48,128]{3,2,1,0:T(8,128)S(1)} %get-tuple-element.15.pad.pad_in), custom_call_target="tpu_custom_call" | custom-call | flops 183500800 | bytes 3670016 | tf_op jit(solution)/shard_map/inner_strips/pallas_call | solution.py:594
  13.9 0.8 %collective-permute-done.4.ea = f32[128,128]{1,0:T(8,128)S(1)} collective-permute-done((f32[128,128]{1,0:T(8,128)S(1)}, f32[128,128]{1,0:T(8,128)S(1)}, u32[]{:S(2)}, u32[]{:S(2)}) %collective-permute-start.4) | collective-permute-done | bytes 65568 | tf_op jit(solution)/shard_map/ppermute | solution.py:35
  14.8 2.2 %assemble.1 = (f32[7,38,48,128]{3,2,1,0:T(8,128)S(1)}, f32[7,2,40,128]{3,2,1,0:T(8,128)S(1)}, f32[7,40,128]{2,1,0:T(8,128)S(1)}) custom-call(f32[7,38,48,128]{3,2,1,0:T(8,128)S(1)} %get-tuple-element.15.pad.pad_in, f32[7,4,2,8,128]{4,3,2,1,0:T(8,128)S(1)} %inner_strips.1.inner, ...), custom_call_target="tpu_custom_call", output_to_operand_aliasing={{0}: (0, {})} | custom-call | tf_op jit(solution)/shard_map/assemble/pallas_call | solution.py:616
  17.0 2.3 %collective-permute-start.6 = (f32[7,40,128]{2,1,0:T(8,128)S(1)}, f32[7,40,128]{2,1,0:T(8,128)S(1)}, u32[]{:S(2)}, u32[]{:S(2)}) collective-permute-start(f32[7,40,128]{2,1,0:T(8,128)S(1)} %get-tuple-element.24), channel_id=1, source_target_pairs={{0,1},{1,0},{2,3},{3,2},{4,5},{5,4},{6,7},{7,6},{8,9},{9,8},{10,11... | collective-permute-start | bytes 430088 | tf_op jit(solution)/shard_map/ppermute | solution.py:35
  19.3 2.8 %plane_faces.1.faces = f32[6,36,48,128]{3,2,1,0:T(8,128)S(1)} custom-call(f32[7,38,48,128]{3,2,1,0:T(8,128)S(1)} %get-tuple-element.22.pad), custom_call_target="tpu_custom_call" | custom-call | flops 262144000 | bytes 3670016 | tf_op jit(solution)/shard_map/plane_faces/pallas_call | solution.py:628
  22.1 0.6 collective-permute-done.6.za
  22.7 15.6 %powers.1 = (bf16[128,192,128]{2,1,0:T(8,128)(2,1)S(1)}, bf16[128,192,128]{2,1,0:T(8,128)(2,1)S(1)}, f32[24,128]{1,0:T(8,128)S(1)}) custom-call(f32[7,38,48,128]{3,2,1,0:T(8,128)S(1)} %get-tuple-element.22.pad, f32[7,2,40,128]{3,2,1,0:T(8,128)S(1)} %get-tuple-element.23.own, f32[6,36,48,128]{3,2,1,0:T(8,128)S(1)} %plane_faces.1.faces, ...), custom_call_target="tpu_custom_call" | custom-call | tf_op jit(solution)/shard_map/powers/pallas_call | solution.py:642
  38.3 2.5 %collective-permute-start.7 = (f32[24,128]{1,0:T(8,128)S(1)}, f32[24,128]{1,0:T(8,128)S(1)}, u32[]{:S(2)}, u32[]{:S(2)}) collective-permute-start(f32[24,128]{1,0:T(8,128)S(1)} %get-tuple-element.25), channel_id=1, source_target_pairs={{0,1},{1,0},{2,3},{3,2},{4,5},{5,4},{6,7},{7,6},{8,9},{9,8},{10,11... | collective-permute-start | bytes 36872 | tf_op jit(solution)/shard_map/ppermute | solution.py:670
  40.8 1.7 %collective-permute-done.7 = f32[24,128]{1,0:T(8,128)S(1)} collective-permute-done((f32[24,128]{1,0:T(8,128)S(1)}, f32[24,128]{1,0:T(8,128)S(1)}, u32[]{:S(2)}, u32[]{:S(2)}) %collective-permute-start.7) | collective-permute-done | bytes 12320 | tf_op jit(solution)/shard_map/ppermute | solution.py:670
  42.5 1.2 %collective-permute-done.8 = f32[24,128]{1,0:T(8,128)S(1)} collective-permute-done((f32[24,128]{1,0:T(8,128)S(1)}, f32[24,128]{1,0:T(8,128)S(1)}, u32[]{:S(2)}, u32[]{:S(2)}) %collective-permute-start.8) | collective-permute-done | bytes 12320 | tf_op jit(solution)/shard_map/ppermute | solution.py:670
  43.6 3.0 %collective-permute-start.9 = (f32[24,128]{1,0:T(8,128)S(1)}, f32[24,128]{1,0:T(8,128)S(1)}, u32[]{:S(2)}, u32[]{:S(2)}) collective-permute-start(f32[24,128]{1,0:T(8,128)S(1)} %add.13), channel_id=1, source_target_pairs={{0,16},{8,24},{16,0},{24,8},{1,17},{9,25},{17,1},{25,9},{2,18},{10... | collective-permute-start | bytes 36872 | tf_op jit(solution)/shard_map/ppermute | solution.py:670
  46.6 1.7 %collective-permute-done.9 = f32[24,128]{1,0:T(8,128)S(1)} collective-permute-done((f32[24,128]{1,0:T(8,128)S(1)}, f32[24,128]{1,0:T(8,128)S(1)}, u32[]{:S(2)}, u32[]{:S(2)}) %collective-permute-start.9) | collective-permute-done | bytes 12320 | tf_op jit(solution)/shard_map/ppermute | solution.py:670
  48.3 4.6 %collective-permute-start.10 = (f32[24,128]{1,0:T(8,128)S(1)}, f32[24,128]{1,0:T(8,128)S(1)}, u32[]{:S(2)}, u32[]{:S(2)}) collective-permute-start(f32[24,128]{1,0:T(8,128)S(1)} %add.14), channel_id=1, source_target_pairs={{0,2},{2,0},{4,6},{6,4},{1,3},{3,1},{5,7},{7,5},{8,10},{10,8},{12,... | collective-permute-start | bytes 36872 | tf_op jit(solution)/shard_map/ppermute | solution.py:670
  52.9 1.7 %collective-permute-done.10 = f32[24,128]{1,0:T(8,128)S(1)} collective-permute-done((f32[24,128]{1,0:T(8,128)S(1)}, f32[24,128]{1,0:T(8,128)S(1)}, u32[]{:S(2)}, u32[]{:S(2)}) %collective-permute-start.10) | collective-permute-done | bytes 12320 | tf_op jit(solution)/shard_map/ppermute | solution.py:670
  54.6 3.6 %collective-permute-start.11 = (f32[24,128]{1,0:T(8,128)S(1)}, f32[24,128]{1,0:T(8,128)S(1)}, u32[]{:S(2)}, u32[]{:S(2)}) collective-permute-start(f32[24,128]{1,0:T(8,128)S(1)} %add.15.gram_a), channel_id=1, source_target_pairs={{0,4},{2,6},{4,0},{6,2},{1,5},{3,7},{5,1},{7,3},{8,12},{10,14},{12... | collective-permute-start | bytes 36872 | tf_op jit(solution)/shard_map/ppermute | solution.py:671
  58.2 1.7 %collective-permute-done.11.gram_b = f32[24,128]{1,0:T(8,128)S(1)} collective-permute-done((f32[24,128]{1,0:T(8,128)S(1)}, f32[24,128]{1,0:T(8,128)S(1)}, u32[]{:S(2)}, u32[]{:S(2)}) %collective-permute-start.11) | collective-permute-done | bytes 12320 | tf_op jit(solution)/shard_map/ppermute | solution.py:671
  59.8 9.2 %factor_and_solve.1 = (f32[24,32,32,128]{3,2,1,0:T(8,128)}, f32[24,24]{1,0:T(8,128)}) custom-call(f32[24,128]{1,0:T(8,128)S(1)} %add.15.gram_a, f32[24,128]{1,0:T(8,128)S(1)} %collective-permute-done.11.gram_b, bf16[128,192,128]{2,1,0:T(8,128)(2,1)S(1)} %get-tuple-element.26.high_ref, bf16[128,192,128]{2,1,0:T(8,128)(2,1)S(1)} %get-tuple-element.27.low_ref), custom_call_target="tpu_custom_call" | custom-call | tf_op jit(solution)/shard_map/factor_and_solve/pallas_call | solution.py:673
  (11 shorter events, 0.1 us)
Async XLA Ops:
  2.7 4.6 %collective-permute-start = (f32[7,3,32,128]{3,2,1,0:T(8,128)S(1)}, f32[7,3,32,128]{3,2,1,0:T(8,128)S(1)}, u32[]{:S(2)}, u32[]{:S(2)}) collective-permute-start(f32[7,3,32,128]{3,2,1,0:T(8,128)S(1)} %get-tuple-element.16), channel_id=1, source_target_pairs={{0,8},{8,0},{16,24},{24,16},{1,9},{9,1},{17,25},{25,17},{2,10},{10... | collective-permute-start | bytes 1032200 | tf_op jit(solution)/shard_map/ppermute | solution.py:35
  3.3 4.0 %collective-permute-start.1 = (f32[7,3,32,128]{3,2,1,0:T(8,128)S(1)}, f32[7,3,32,128]{3,2,1,0:T(8,128)S(1)}, u32[]{:S(2)}, u32[]{:S(2)}) collective-permute-start(f32[7,3,32,128]{3,2,1,0:T(8,128)S(1)} %get-tuple-element.17), channel_id=1, source_target_pairs={{8,16},{16,8},{9,17},{17,9},{10,18},{18,10},{11,19},{19,11},{12,20... | collective-permute-start | bytes 1032200 | tf_op jit(solution)/shard_map/ppermute | solution.py:38
  4.0 9.9 %collective-permute-start.2 = (f32[672,128]{1,0:T(8,128)S(1)}, f32[672,128]{1,0:T(8,128)S(1)}, u32[]{:S(2)}, u32[]{:S(2)}) collective-permute-start(f32[672,128]{1,0:T(8,128)S(1)} %get-tuple-element.18), channel_id=1, source_target_pairs={{0,2},{2,0},{4,6},{6,4},{1,3},{3,1},{5,7},{7,5},{8,10},{10,8},{12,... | collective-permute-start | bytes 1032200 | tf_op jit(solution)/shard_map/ppermute | solution.py:35
  6.6 7.3 %collective-permute-start.3 = (f32[672,128]{1,0:T(8,128)S(1)}, f32[672,128]{1,0:T(8,128)S(1)}, u32[]{:S(2)}, u32[]{:S(2)}) collective-permute-start(f32[672,128]{1,0:T(8,128)S(1)} %get-tuple-element.19), channel_id=1, source_target_pairs={{2,4},{4,2},{3,5},{5,3},{10,12},{12,10},{11,13},{13,11},{18,20},{2... | collective-permute-start | bytes 1032200 | tf_op jit(solution)/shard_map/ppermute | solution.py:38
  7.4 7.4 %collective-permute-start.4 = (f32[128,128]{1,0:T(8,128)S(1)}, f32[128,128]{1,0:T(8,128)S(1)}, u32[]{:S(2)}, u32[]{:S(2)}) collective-permute-start(f32[128,128]{1,0:T(8,128)S(1)} %get-tuple-element.20), channel_id=1, source_target_pairs={{0,2},{2,0},{4,6},{6,4},{1,3},{3,1},{5,7},{7,5},{8,10},{10,8},{12,... | collective-permute-start | bytes 196616 | tf_op jit(solution)/shard_map/ppermute | solution.py:35
  11.8 2.9 %collective-permute-start.5 = (f32[128,128]{1,0:T(8,128)S(1)}, f32[128,128]{1,0:T(8,128)S(1)}, u32[]{:S(2)}, u32[]{:S(2)}) collective-permute-start(f32[128,128]{1,0:T(8,128)S(1)} %get-tuple-element.21), channel_id=1, source_target_pairs={{2,4},{4,2},{3,5},{5,3},{10,12},{12,10},{11,13},{13,11},{18,20},{2... | collective-permute-start | bytes 196616 | tf_op jit(solution)/shard_map/ppermute | solution.py:38
  17.0 5.7 %collective-permute-start.6 = (f32[7,40,128]{2,1,0:T(8,128)S(1)}, f32[7,40,128]{2,1,0:T(8,128)S(1)}, u32[]{:S(2)}, u32[]{:S(2)}) collective-permute-start(f32[7,40,128]{2,1,0:T(8,128)S(1)} %get-tuple-element.24), channel_id=1, source_target_pairs={{0,1},{1,0},{2,3},{3,2},{4,5},{5,4},{6,7},{7,6},{8,9},{9,8},{10,11... | collective-permute-start | bytes 430088 | tf_op jit(solution)/shard_map/ppermute | solution.py:35
  38.3 4.2 %collective-permute-start.7 = (f32[24,128]{1,0:T(8,128)S(1)}, f32[24,128]{1,0:T(8,128)S(1)}, u32[]{:S(2)}, u32[]{:S(2)}) collective-permute-start(f32[24,128]{1,0:T(8,128)S(1)} %get-tuple-element.25), channel_id=1, source_target_pairs={{0,1},{1,0},{2,3},{3,2},{4,5},{5,4},{6,7},{7,6},{8,9},{9,8},{10,11... | collective-permute-start | bytes 36872 | tf_op jit(solution)/shard_map/ppermute | solution.py:670
  42.4 1.2 %collective-permute-start.8 = (f32[24,128]{1,0:T(8,128)S(1)}, f32[24,128]{1,0:T(8,128)S(1)}, u32[]{:S(2)}, u32[]{:S(2)}) collective-permute-start(f32[24,128]{1,0:T(8,128)S(1)} %add.12), channel_id=1, source_target_pairs={{0,8},{8,0},{16,24},{24,16},{1,9},{9,1},{17,25},{25,17},{2,10},{10... | collective-permute-start | bytes 36872 | tf_op jit(solution)/shard_map/ppermute | solution.py:670
  43.6 4.7 %collective-permute-start.9 = (f32[24,128]{1,0:T(8,128)S(1)}, f32[24,128]{1,0:T(8,128)S(1)}, u32[]{:S(2)}, u32[]{:S(2)}) collective-permute-start(f32[24,128]{1,0:T(8,128)S(1)} %add.13), channel_id=1, source_target_pairs={{0,16},{8,24},{16,0},{24,8},{1,17},{9,25},{17,1},{25,9},{2,18},{10... | collective-permute-start | bytes 36872 | tf_op jit(solution)/shard_map/ppermute | solution.py:670
  48.3 6.3 %collective-permute-start.10 = (f32[24,128]{1,0:T(8,128)S(1)}, f32[24,128]{1,0:T(8,128)S(1)}, u32[]{:S(2)}, u32[]{:S(2)}) collective-permute-start(f32[24,128]{1,0:T(8,128)S(1)} %add.14), channel_id=1, source_target_pairs={{0,2},{2,0},{4,6},{6,4},{1,3},{3,1},{5,7},{7,5},{8,10},{10,8},{12,... | collective-permute-start | bytes 36872 | tf_op jit(solution)/shard_map/ppermute | solution.py:670
  54.6 5.3 %collective-permute-start.11 = (f32[24,128]{1,0:T(8,128)S(1)}, f32[24,128]{1,0:T(8,128)S(1)}, u32[]{:S(2)}, u32[]{:S(2)}) collective-permute-start(f32[24,128]{1,0:T(8,128)S(1)} %add.15.gram_a), channel_id=1, source_target_pairs={{0,4},{2,6},{4,0},{6,2},{1,5},{3,7},{5,1},{7,3},{8,12},{10,14},{12... | collective-permute-start | bytes 36872 | tf_op jit(solution)/shard_map/ppermute | solution.py:671

commit v5 on v4

--- a/solution.py
+++ b/solution.py
@@ -71,22 +71,22 @@
             yb_ref[row : row + DEPTH, :] = jnp.where(ey, low, high)
 
 
+CORNERS = ((1, 1), (1, 2), (2, 1))
+
+
 def pack_edges(xa_ref, xb_ref, ea_ref, eb_ref):
     fields, _, ny, _ = xa_ref.shape
     ex, ey = even_on("gx"), even_on("gy")
     for f in range(fields):
         for side in range(2):
-            for i in range(DEPTH):
-                a, b = xa_ref, xb_ref
-                if side == 0:
-                    low = jnp.where(ex, b[f, i, :DEPTH, :], a[f, i, :DEPTH, :])
-                    high = jnp.where(ex, b[f, i, ny - DEPTH :, :], a[f, i, ny - DEPTH :, :])
-                else:
-                    low = jnp.where(ex, a[f, i, :DEPTH, :], b[f, i, :DEPTH, :])
-                    high = jnp.where(ex, a[f, i, ny - DEPTH :, :], b[f, i, ny - DEPTH :, :])
-                row = DEPTH * ((f * 2 + side) * DEPTH + i)
-                ea_ref[row : row + DEPTH, :] = jnp.where(ey, high, low)
-                eb_ref[row : row + DEPTH, :] = jnp.where(ey, low, high)
+            a, b = (xa_ref, xb_ref) if side == 0 else (xb_ref, xa_ref)
+            for c, (dx, dy) in enumerate(CORNERS):
+                i = DEPTH - dx if side == 0 else dx - 1
+                low = jnp.where(ex, b[f, i, dy - 1 : dy, :], a[f, i, dy - 1 : dy, :])
+                high = jnp.where(ex, b[f, i, ny - dy : ny - dy + 1, :], a[f, i, ny - dy : ny - dy + 1, :])
+                row = len(CORNERS) * (2 * f + side) + c
+                ea_ref[row : row + 1, :] = jnp.where(ey, high, low)
+                eb_ref[row : row + 1, :] = jnp.where(ey, low, high)
 
 
 def assemble(nx, ny, two_z, pad_in, inner, xa, xb, ya, yb, ea, eb, *outs):
@@ -112,13 +112,18 @@
             a, b = ya[row : row + DEPTH, :], yb[row : row + DEPTH, :]
             pad[f, x + DEPTH, TOP - DEPTH : TOP, :] = jnp.where(ey, b, a)
             pad[f, x + DEPTH, bottom : bottom + DEPTH, :] = jnp.where(ey, a, b)
+        empty = jnp.zeros((DEPTH, LANES), F32)
         for side in range(2):
             for i in range(DEPTH):
-                row = DEPTH * ((f * 2 + side) * DEPTH + i)
                 plane = i if side == 0 else nx + DEPTH + i
-                a, b = ea[row : row + DEPTH, :], eb[row : row + DEPTH, :]
-                pad[f, plane, TOP - DEPTH : TOP, :] = jnp.where(ey, b, a)
-                pad[f, plane, bottom : bottom + DEPTH, :] = jnp.where(ey, a, b)
+                pad[f, plane, TOP - DEPTH : TOP, :] = empty
+                pad[f, plane, bottom : bottom + DEPTH, :] = empty
+            for c, (dx, dy) in enumerate(CORNERS):
+                plane = DEPTH - dx if side == 0 else nx + DEPTH - 1 + dx
+                row = len(CORNERS) * (2 * f + side) + c
+                a, b = ea[row : row + 1, :], eb[row : row + 1, :]
+                pad[f, plane, TOP - dy : TOP - dy + 1, :] = jnp.where(ey, b, a)
+                pad[f, plane, bottom + dy - 1 : bottom + dy, :] = jnp.where(ey, a, b)
 
     lane = lane_index()
     place = lane // 2
@@ -578,7 +583,7 @@
     pad_type = pltpu.VMEM((slabs, wide, tall, LANES), F32)
     x_type = pltpu.VMEM((slabs, DEPTH, ny, LANES), F32)
     y_type = pltpu.VMEM((slabs * nx * DEPTH, LANES), F32)
-    e_rows = 8 * ((slabs * 2 * DEPTH * DEPTH + 7) // 8)
+    e_rows = 8 * ((slabs * 2 * len(CORNERS) + 7) // 8)
     e_type = pltpu.VMEM((e_rows, LANES), F32)
     pad, xa, xb, ya, yb = pl.pallas_call(
         pack_faces,

time: 69.2 us -> 68.7 us (level)
  waiting for transfers between devices: 9.31 us -> 7.8 us
  starting transfers between devices: 25.6 us -> 26.6 us
    ppermute x4, waiting for transfers between devices: 1.43 us -> 0.27 us  [pair_exchange(): lax.ppermute(first, axis, [p for a, b in firsts for p in ((a, b), (b, a))])]
    ppermute x4, starting transfers between devices: 10.1 us -> 11.2 us  [on_device(): gram = gram + lax.ppermute(gram, axis, pairs)]
  transfers between devices with their start and end apart: 12 -> 12, of which waited for: 7 -> 6; matrix products, arithmetic and copies ran while one was open for 0% -> 0% of each run, Pallas kernels for 6% -> 6%
where the time goes in v5:
time: 68.7 us; the launch traced here: 68.5 us
  Pallas kernels  33.4 us (49%)
  starting transfers between devices  26.6 us (39%)
  waiting for transfers between devices  7.8 us (11%)
  between operations  0.74 us (1%)
    pallas_call x1, Pallas kernels, on_device(): pl.pallas_call(functools.partial(powers, nx, ny, two_z), out_shape=(split...  15.6 us
    ppermute x4, starting transfers between devices, on_device(): gram = gram + lax.ppermute(gram, axis, pairs)  11.2 us
    ppermute x4, starting transfers between devices, pair_exchange(): lax.ppermute(first, axis, [p for a, b in firsts for p in ((a, b), (b, a))])  9.87 us
    pallas_call x1, Pallas kernels, on_device(): pl.pallas_call(functools.partial(factor_and_solve, cells, order, nx, ny),...  9.17 us
    ppermute x4, waiting for transfers between devices, on_device(): gram = gram + lax.ppermute(gram, axis, pairs)  5.85 us
    ppermute x1, starting transfers between devices, on_device(): other = lax.ppermute(gram, *stages[-1])  3.47 us
    pallas_call x1, Pallas kernels, on_device(): pl.pallas_call(functools.partial(plane_faces, nx, ny), out_shape=pltpu.VM...  2.82 us
    pallas_call x1, Pallas kernels, on_device(): pl.pallas_call(functools.partial(assemble, nx, ny, two_z), out_shape=(pad...  2.25 us
  transfers between devices with their start and end apart: 12, of which 6 were waited for; matrix products, arithmetic and copies ran while one was open for 0% of the time, Pallas kernels for 6%

profile of v5, /device:TPU:0, one launch (start us, length us, event | category | flops | bytes accessed | tf_op | source)
XLA Modules:
  0.0 68.5 jit_solution(5207119502173853047)
XLA Ops:
  0.6 2.1 %pack_faces.1 = (f32[7,38,48,128]{3,2,1,0:T(8,128)S(1)}, f32[7,3,32,128]{3,2,1,0:T(8,128)S(1)}, f32[7,3,32,128]{3,2,1,0:T(8,128)S(1)}, f32[672,128]{1,0:T(8,128)S(1)}, f32[672,128]{1,0:T(8,128)S(1)}) custom-call(f32[6,32,32,128]{3,2,1,0:T(8,128)} %rs_ref.1, f32[32,32,128]{2,1,0:T(8,128)} %k_ref.1), custom_call_target="tpu_custom_call" | custom-call | tf_op jit(solution)/shard_map/pack_faces/pallas_call | solution.py:588
  2.7 0.6 collective-permute-start
  3.3 0.7 collective-permute-start.1
  4.0 2.6 %collective-permute-start.2 = (f32[672,128]{1,0:T(8,128)S(1)}, f32[672,128]{1,0:T(8,128)S(1)}, u32[]{:S(2)}, u32[]{:S(2)}) collective-permute-start(f32[672,128]{1,0:T(8,128)S(1)} %get-tuple-element.18), channel_id=1, source_target_pairs={{0,2},{2,0},{4,6},{6,4},{1,3},{3,1},{5,7},{7,5},{8,10},{10,8},{12,... | collective-permute-start | bytes 1032200 | tf_op jit(solution)/shard_map/ppermute | solution.py:35
  6.6 0.7 collective-permute-start.3
  7.4 4.4 %collective-permute-start.4 = (f32[48,128]{1,0:T(8,128)S(1)}, f32[48,128]{1,0:T(8,128)S(1)}, u32[]{:S(2)}, u32[]{:S(2)}) collective-permute-start(f32[48,128]{1,0:T(8,128)S(1)} %get-tuple-element.20), channel_id=1, source_target_pairs={{0,2},{2,0},{4,6},{6,4},{1,3},{3,1},{5,7},{7,5},{8,10},{10,8},{12,... | collective-permute-start | bytes 73736 | tf_op jit(solution)/shard_map/ppermute | solution.py:35
  11.8 0.7 collective-permute-start.5
  12.5 1.4 %inner_strips.1.inner = f32[7,4,2,8,128]{4,3,2,1,0:T(8,128)S(1)} custom-call(f32[7,38,48,128]{3,2,1,0:T(8,128)S(1)} %get-tuple-element.15.pad.pad_in), custom_call_target="tpu_custom_call" | custom-call | flops 183500800 | bytes 3670016 | tf_op jit(solution)/shard_map/inner_strips/pallas_call | solution.py:599
  13.9 2.2 %assemble.1 = (f32[7,38,48,128]{3,2,1,0:T(8,128)S(1)}, f32[7,2,40,128]{3,2,1,0:T(8,128)S(1)}, f32[7,40,128]{2,1,0:T(8,128)S(1)}) custom-call(f32[7,38,48,128]{3,2,1,0:T(8,128)S(1)} %get-tuple-element.15.pad.pad_in, f32[7,4,2,8,128]{4,3,2,1,0:T(8,128)S(1)} %inner_strips.1.inner, ...), custom_call_target="tpu_custom_call", output_to_operand_aliasing={{0}: (0, {})} | custom-call | tf_op jit(solution)/shard_map/assemble/pallas_call | solution.py:621
  16.2 2.2 %collective-permute-start.6 = (f32[7,40,128]{2,1,0:T(8,128)S(1)}, f32[7,40,128]{2,1,0:T(8,128)S(1)}, u32[]{:S(2)}, u32[]{:S(2)}) collective-permute-start(f32[7,40,128]{2,1,0:T(8,128)S(1)} %get-tuple-element.24), channel_id=1, source_target_pairs={{0,1},{1,0},{2,3},{3,2},{4,5},{5,4},{6,7},{7,6},{8,9},{9,8},{10,11... | collective-permute-start | bytes 430088 | tf_op jit(solution)/shard_map/ppermute | solution.py:35
  18.4 2.8 %plane_faces.1.faces = f32[6,36,48,128]{3,2,1,0:T(8,128)S(1)} custom-call(f32[7,38,48,128]{3,2,1,0:T(8,128)S(1)} %get-tuple-element.22.pad), custom_call_target="tpu_custom_call" | custom-call | flops 262144000 | bytes 3670016 | tf_op jit(solution)/shard_map/plane_faces/pallas_call | solution.py:633
  21.2 0.3 collective-permute-done.6.za
  21.5 15.6 %powers.1 = (bf16[128,192,128]{2,1,0:T(8,128)(2,1)S(1)}, bf16[128,192,128]{2,1,0:T(8,128)(2,1)S(1)}, f32[24,128]{1,0:T(8,128)S(1)}) custom-call(f32[7,38,48,128]{3,2,1,0:T(8,128)S(1)} %get-tuple-element.22.pad, f32[7,2,40,128]{3,2,1,0:T(8,128)S(1)} %get-tuple-element.23.own, f32[6,36,48,128]{3,2,1,0:T(8,128)S(1)} %plane_faces.1.faces, ...), custom_call_target="tpu_custom_call" | custom-call | tf_op jit(solution)/shard_map/powers/pallas_call | solution.py:647
  37.1 2.0 %collective-permute-start.7 = (f32[24,128]{1,0:T(8,128)S(1)}, f32[24,128]{1,0:T(8,128)S(1)}, u32[]{:S(2)}, u32[]{:S(2)}) collective-permute-start(f32[24,128]{1,0:T(8,128)S(1)} %get-tuple-element.25), channel_id=1, source_target_pairs={{0,1},{1,0},{2,3},{3,2},{4,5},{5,4},{6,7},{7,6},{8,9},{9,8},{10,11... | collective-permute-start | bytes 36872 | tf_op jit(solution)/shard_map/ppermute | solution.py:675
  39.1 1.7 %collective-permute-done.7 = f32[24,128]{1,0:T(8,128)S(1)} collective-permute-done((f32[24,128]{1,0:T(8,128)S(1)}, f32[24,128]{1,0:T(8,128)S(1)}, u32[]{:S(2)}, u32[]{:S(2)}) %collective-permute-start.7) | collective-permute-done | bytes 12320 | tf_op jit(solution)/shard_map/ppermute | solution.py:675
  40.8 0.9 %collective-permute-start.8 = (f32[24,128]{1,0:T(8,128)S(1)}, f32[24,128]{1,0:T(8,128)S(1)}, u32[]{:S(2)}, u32[]{:S(2)}) collective-permute-start(f32[24,128]{1,0:T(8,128)S(1)} %add.12), channel_id=1, source_target_pairs={{0,8},{8,0},{16,24},{24,16},{1,9},{9,1},{17,25},{25,17},{2,10},{10... | collective-permute-start | bytes 36872 | tf_op jit(solution)/shard_map/ppermute | solution.py:675
  41.7 0.8 %collective-permute-done.8 = f32[24,128]{1,0:T(8,128)S(1)} collective-permute-done((f32[24,128]{1,0:T(8,128)S(1)}, f32[24,128]{1,0:T(8,128)S(1)}, u32[]{:S(2)}, u32[]{:S(2)}) %collective-permute-start.8) | collective-permute-done | bytes 12320 | tf_op jit(solution)/shard_map/ppermute | solution.py:675
  42.5 3.7 %collective-permute-start.9 = (f32[24,128]{1,0:T(8,128)S(1)}, f32[24,128]{1,0:T(8,128)S(1)}, u32[]{:S(2)}, u32[]{:S(2)}) collective-permute-start(f32[24,128]{1,0:T(8,128)S(1)} %add.13), channel_id=1, source_target_pairs={{0,16},{8,24},{16,0},{24,8},{1,17},{9,25},{17,1},{25,9},{2,18},{10... | collective-permute-start | bytes 36872 | tf_op jit(solution)/shard_map/ppermute | solution.py:675
  46.2 1.7 %collective-permute-done.9 = f32[24,128]{1,0:T(8,128)S(1)} collective-permute-done((f32[24,128]{1,0:T(8,128)S(1)}, f32[24,128]{1,0:T(8,128)S(1)}, u32[]{:S(2)}, u32[]{:S(2)}) %collective-permute-start.9) | collective-permute-done | bytes 12320 | tf_op jit(solution)/shard_map/ppermute | solution.py:675
  47.9 4.6 %collective-permute-start.10 = (f32[24,128]{1,0:T(8,128)S(1)}, f32[24,128]{1,0:T(8,128)S(1)}, u32[]{:S(2)}, u32[]{:S(2)}) collective-permute-start(f32[24,128]{1,0:T(8,128)S(1)} %add.14), channel_id=1, source_target_pairs={{0,2},{2,0},{4,6},{6,4},{1,3},{3,1},{5,7},{7,5},{8,10},{10,8},{12,... | collective-permute-start | bytes 36872 | tf_op jit(solution)/shard_map/ppermute | solution.py:675
  52.5 1.7 %collective-permute-done.10 = f32[24,128]{1,0:T(8,128)S(1)} collective-permute-done((f32[24,128]{1,0:T(8,128)S(1)}, f32[24,128]{1,0:T(8,128)S(1)}, u32[]{:S(2)}, u32[]{:S(2)}) %collective-permute-start.10) | collective-permute-done | bytes 12320 | tf_op jit(solution)/shard_map/ppermute | solution.py:675
  54.2 3.5 %collective-permute-start.11 = (f32[24,128]{1,0:T(8,128)S(1)}, f32[24,128]{1,0:T(8,128)S(1)}, u32[]{:S(2)}, u32[]{:S(2)}) collective-permute-start(f32[24,128]{1,0:T(8,128)S(1)} %add.15.gram_a), channel_id=1, source_target_pairs={{0,4},{2,6},{4,0},{6,2},{1,5},{3,7},{5,1},{7,3},{8,12},{10,14},{12... | collective-permute-start | bytes 36872 | tf_op jit(solution)/shard_map/ppermute | solution.py:676
  57.6 1.7 %collective-permute-done.11.gram_b = f32[24,128]{1,0:T(8,128)S(1)} collective-permute-done((f32[24,128]{1,0:T(8,128)S(1)}, f32[24,128]{1,0:T(8,128)S(1)}, u32[]{:S(2)}, u32[]{:S(2)}) %collective-permute-start.11) | collective-permute-done | bytes 12320 | tf_op jit(solution)/shard_map/ppermute | solution.py:676
  59.3 9.2 %factor_and_solve.1 = (f32[24,32,32,128]{3,2,1,0:T(8,128)}, f32[24,24]{1,0:T(8,128)}) custom-call(f32[24,128]{1,0:T(8,128)S(1)} %add.15.gram_a, f32[24,128]{1,0:T(8,128)S(1)} %collective-permute-done.11.gram_b, bf16[128,192,128]{2,1,0:T(8,128)(2,1)S(1)} %get-tuple-element.26.high_ref, bf16[128,192,128]{2,1,0:T(8,128)(2,1)S(1)} %get-tuple-element.27.low_ref), custom_call_target="tpu_custom_call" | custom-call | tf_op jit(solution)/shard_map/factor_and_solve/pallas_call | solution.py:678
  (11 shorter events, 0.1 us)
Async XLA Ops:
  2.7 4.6 %collective-permute-start = (f32[7,3,32,128]{3,2,1,0:T(8,128)S(1)}, f32[7,3,32,128]{3,2,1,0:T(8,128)S(1)}, u32[]{:S(2)}, u32[]{:S(2)}) collective-permute-start(f32[7,3,32,128]{3,2,1,0:T(8,128)S(1)} %get-tuple-element.16), channel_id=1, source_target_pairs={{0,8},{8,0},{16,24},{24,16},{1,9},{9,1},{17,25},{25,17},{2,10},{10... | collective-permute-start | bytes 1032200 | tf_op jit(solution)/shard_map/ppermute | solution.py:35
  3.3 4.0 %collective-permute-start.1 = (f32[7,3,32,128]{3,2,1,0:T(8,128)S(1)}, f32[7,3,32,128]{3,2,1,0:T(8,128)S(1)}, u32[]{:S(2)}, u32[]{:S(2)}) collective-permute-start(f32[7,3,32,128]{3,2,1,0:T(8,128)S(1)} %get-tuple-element.17), channel_id=1, source_target_pairs={{8,16},{16,8},{9,17},{17,9},{10,18},{18,10},{11,19},{19,11},{12,20... | collective-permute-start | bytes 1032200 | tf_op jit(solution)/shard_map/ppermute | solution.py:38
  4.0 9.9 %collective-permute-start.2 = (f32[672,128]{1,0:T(8,128)S(1)}, f32[672,128]{1,0:T(8,128)S(1)}, u32[]{:S(2)}, u32[]{:S(2)}) collective-permute-start(f32[672,128]{1,0:T(8,128)S(1)} %get-tuple-element.18), channel_id=1, source_target_pairs={{0,2},{2,0},{4,6},{6,4},{1,3},{3,1},{5,7},{7,5},{8,10},{10,8},{12,... | collective-permute-start | bytes 1032200 | tf_op jit(solution)/shard_map/ppermute | solution.py:35
  6.6 7.3 %collective-permute-start.3 = (f32[672,128]{1,0:T(8,128)S(1)}, f32[672,128]{1,0:T(8,128)S(1)}, u32[]{:S(2)}, u32[]{:S(2)}) collective-permute-start(f32[672,128]{1,0:T(8,128)S(1)} %get-tuple-element.19), channel_id=1, source_target_pairs={{2,4},{4,2},{3,5},{5,3},{10,12},{12,10},{11,13},{13,11},{18,20},{2... | collective-permute-start | bytes 1032200 | tf_op jit(solution)/shard_map/ppermute | solution.py:38
  7.4 6.6 %collective-permute-start.4 = (f32[48,128]{1,0:T(8,128)S(1)}, f32[48,128]{1,0:T(8,128)S(1)}, u32[]{:S(2)}, u32[]{:S(2)}) collective-permute-start(f32[48,128]{1,0:T(8,128)S(1)} %get-tuple-element.20), channel_id=1, source_target_pairs={{0,2},{2,0},{4,6},{6,4},{1,3},{3,1},{5,7},{7,5},{8,10},{10,8},{12,... | collective-permute-start | bytes 73736 | tf_op jit(solution)/shard_map/ppermute | solution.py:35
  11.8 2.1 %collective-permute-start.5 = (f32[48,128]{1,0:T(8,128)S(1)}, f32[48,128]{1,0:T(8,128)S(1)}, u32[]{:S(2)}, u32[]{:S(2)}) collective-permute-start(f32[48,128]{1,0:T(8,128)S(1)} %get-tuple-element.21), channel_id=1, source_target_pairs={{2,4},{4,2},{3,5},{5,3},{10,12},{12,10},{11,13},{13,11},{18,20},{2... | collective-permute-start | bytes 73736 | tf_op jit(solution)/shard_map/ppermute | solution.py:38
  16.2 5.3 %collective-permute-start.6 = (f32[7,40,128]{2,1,0:T(8,128)S(1)}, f32[7,40,128]{2,1,0:T(8,128)S(1)}, u32[]{:S(2)}, u32[]{:S(2)}) collective-permute-start(f32[7,40,128]{2,1,0:T(8,128)S(1)} %get-tuple-element.24), channel_id=1, source_target_pairs={{0,1},{1,0},{2,3},{3,2},{4,5},{5,4},{6,7},{7,6},{8,9},{9,8},{10,11... | collective-permute-start | bytes 430088 | tf_op jit(solution)/shard_map/ppermute | solution.py:35
  37.1 3.7 %collective-permute-start.7 = (f32[24,128]{1,0:T(8,128)S(1)}, f32[24,128]{1,0:T(8,128)S(1)}, u32[]{:S(2)}, u32[]{:S(2)}) collective-permute-start(f32[24,128]{1,0:T(8,128)S(1)} %get-tuple-element.25), channel_id=1, source_target_pairs={{0,1},{1,0},{2,3},{3,2},{4,5},{5,4},{6,7},{7,6},{8,9},{9,8},{10,11... | collective-permute-start | bytes 36872 | tf_op jit(solution)/shard_map/ppermute | solution.py:675
  40.8 1.7 %collective-permute-start.8 = (f32[24,128]{1,0:T(8,128)S(1)}, f32[24,128]{1,0:T(8,128)S(1)}, u32[]{:S(2)}, u32[]{:S(2)}) collective-permute-start(f32[24,128]{1,0:T(8,128)S(1)} %add.12), channel_id=1, source_target_pairs={{0,8},{8,0},{16,24},{24,16},{1,9},{9,1},{17,25},{25,17},{2,10},{10... | collective-permute-start | bytes 36872 | tf_op jit(solution)/shard_map/ppermute | solution.py:675
  42.5 5.4 %collective-permute-start.9 = (f32[24,128]{1,0:T(8,128)S(1)}, f32[24,128]{1,0:T(8,128)S(1)}, u32[]{:S(2)}, u32[]{:S(2)}) collective-permute-start(f32[24,128]{1,0:T(8,128)S(1)} %add.13), channel_id=1, source_target_pairs={{0,16},{8,24},{16,0},{24,8},{1,17},{9,25},{17,1},{25,9},{2,18},{10... | collective-permute-start | bytes 36872 | tf_op jit(solution)/shard_map/ppermute | solution.py:675
  47.9 6.3 %collective-permute-start.10 = (f32[24,128]{1,0:T(8,128)S(1)}, f32[24,128]{1,0:T(8,128)S(1)}, u32[]{:S(2)}, u32[]{:S(2)}) collective-permute-start(f32[24,128]{1,0:T(8,128)S(1)} %add.14), channel_id=1, source_target_pairs={{0,2},{2,0},{4,6},{6,4},{1,3},{3,1},{5,7},{7,5},{8,10},{10,8},{12,... | collective-permute-start | bytes 36872 | tf_op jit(solution)/shard_map/ppermute | solution.py:675
  54.2 5.1 %collective-permute-start.11 = (f32[24,128]{1,0:T(8,128)S(1)}, f32[24,128]{1,0:T(8,128)S(1)}, u32[]{:S(2)}, u32[]{:S(2)}) collective-permute-start(f32[24,128]{1,0:T(8,128)S(1)} %add.15.gram_a), channel_id=1, source_target_pairs={{0,4},{2,6},{4,0},{6,2},{1,5},{3,7},{5,1},{7,3},{8,12},{10,14},{12... | collective-permute-start | bytes 36872 | tf_op jit(solution)/shard_map/ppermute | solution.py:676
